TPU v7x, 32 devices: a whole 2x2x4 slice. The times are simulated.
32 devices in a mesh: seq: 16 (over z, y, x), head: 2 (over core).
Axes of the slice: x: 2, y: 2, z: 4, core: 2. Of those that a mesh axis runs over, the one named last changes fastest.
Arguments:
- hidden: bfloat16 [8192, 1536], P('seq'), may hold values from -6 to 6
- cotangent: bfloat16 [8192, 1536], P('seq'), may hold values from -6 to 6
- z_proj: bfloat16 [1536, 3072], P('seq', 'head'), may hold values from -0.15625 to 0.15625
- x_proj: bfloat16 [1536, 3072], P('seq', 'head'), may hold values from -0.15625 to 0.15625
- bc_proj: bfloat16 [1536, 256], P('seq', 'head'), may hold values from -0.15625 to 0.15625
- dt_proj: bfloat16 [1536, 48], P('seq', 'head'), may hold values from -0.15625 to 0.15625
- out_proj: bfloat16 [1536, 3072], P('seq', 'head'), may hold values from -0.109375 to 0.109375
- conv_x: float32 [4, 3072], P(None, 'head'), may hold values from -2 to 2
- conv_x_bias: float32 [3072], P('head'), may hold values from -2 to 2
- conv_bc: float32 [4, 256], P(None, 'head'), may hold values from -2 to 2
- conv_bc_bias: float32 [256], P('head'), may hold values from -2 to 2
- dt_bias: float32 [48], P('head'), may hold values from -9 to -1
- a_log: float32 [48], P('head'), may hold values from -2.5 to 0.5
- d_skip: float32 [48], P('head'), may hold values from 0.5 to 1.5
- norm_gain: float32 [1536], replicated, may hold values from 0.1 to 1.9
- gate_gain: float32 [3072], P('head'), may hold values from 0.1 to 1.9
- lengths: int32 [2, 8], replicated, may hold values from 1 to 4, 16 in all within a row
- dealing: int32 [2, 16], replicated, may hold values from 0 to 15, each once within a row
Outputs:
- block_out: bfloat16 [8192, 1536], P('seq', 'head')
- grad_hidden: float32 [8192, 1536], P('seq', 'head')
- grad_z_proj: float32 [1536, 3072], P('seq', 'head')
- grad_x_proj: float32 [1536, 3072], P('seq', 'head')
- grad_bc_proj: float32 [1536, 256], P('seq', 'head')
- grad_dt_proj: float32 [1536, 48], P('seq', 'head')
- grad_out_proj: float32 [1536, 3072], P('seq', 'head')
- grad_conv_x: float32 [4, 3072], P(None, 'head')
- grad_conv_x_bias: float32 [3072], P('head')
- grad_conv_bc: float32 [4, 256], P(None, 'head')
- grad_conv_bc_bias: float32 [256], P('head')
- grad_dt_bias: float32 [48], P('head')
- grad_a_log: float32 [48], P('head')
- grad_d_skip: float32 [48], P('head')
- grad_norm_gain: float32 [1536], P('head')
- grad_gate_gain: float32 [3072], P('head')
Inputs may be any that keep to these rules, and one draw needn't show every extreme that they name: `lengths`: each row sums to 16 runs of 256 rows; its largest entry is 4. `dealing`: each row is a permutation of the seq indices.
All inputs are finite; a program needn't handle non-finite values.
Results may differ from a plain program's by a relative error of at most 0.02.
Values may be sent and summed in bfloat16 or wider, within the bound.
No kernel may reach another device: no remote copies, remote signals or barrier semaphores. Data moves between devices by JAX's collectives and lax.ppermute only.
A program may use at most 192 MiB of HBM per device.

v0:
```python
import jax
import jax.numpy as jnp
from jax import lax
from jax.sharding import PartitionSpec as P

MODEL_WIDTH = 1536
HDIM = 64
STATE = 128
BLOCK = 256
INNER = 3072


EPSILON = 1e-05
HIGHEST = lax.Precision.HIGHEST


def silu_grad(value):
    sigmoid_v = jax.nn.sigmoid(value)
    return sigmoid_v * (1.0 + value * (1.0 - sigmoid_v))


def contract_rows(left_op, right_op):
    return lax.dot_general(
        left_op, right_op, (((0,), (0,)), ((), ())), preferred_element_type=jnp.float32
    )


def contract_cols(left_op, right_op):
    return lax.dot_general(
        left_op, right_op, (((1,), (1,)), ((), ())), preferred_element_type=jnp.float32
    )


def split_parts(value):
    if value.dtype == jnp.bfloat16:
        return (value,)
    upper_part = value.astype(jnp.bfloat16)
    lower_part = (value - upper_part.astype(jnp.float32)).astype(jnp.bfloat16)
    return (upper_part, lower_part)


def mixed_einsum(form, left_op, right_op):
    left_parts = split_parts(left_op)
    right_parts = split_parts(right_op)
    summed_up = None
    for left_at in range(len(left_parts)):
        for right_at in range(len(right_parts)):
            if left_at + right_at < 2:
                product_term = jnp.einsum(
                    form,
                    left_parts[left_at],
                    right_parts[right_at],
                    preferred_element_type=jnp.float32,
                )
                summed_up = product_term if summed_up is None else summed_up + product_term
    return summed_up


def scatter_rows(term_fn, own_rows):
    return lax.psum_scatter(
        term_fn(jnp.int32(0), own_rows * lax.axis_size("seq")).astype(jnp.bfloat16),
        "seq",
        scatter_dimension=0,
        tiled=True,
    ).astype(jnp.float32)


def per_device(
    hidden,
    cotangent,
    z_proj,
    x_proj,
    bc_proj,
    dt_proj,
    out_proj,
    conv_x,
    conv_x_bias,
    conv_bc,
    conv_bc_bias,
    dt_bias,
    a_log,
    d_skip,
    norm_gain,
    gate_gain,
    lengths,
    dealing,
):
    n_seq = lax.axis_size("seq")
    n_head = lax.axis_size("head")
    seq_at = lax.axis_index("seq")
    head_offset = lax.axis_index("head")
    micro_count = lengths.shape[0]
    run_count = dealing.shape[1]
    run_len = hidden.shape[0] // micro_count
    portion_length = MODEL_WIDTH // n_head
    inner_loc = z_proj.shape[1]
    bc_loc = bc_proj.shape[1]
    heads_loc = dt_proj.shape[1]
    n_blocks = run_len // BLOCK
    own_rows = MODEL_WIDTH // n_seq
    width_in = 2 * inner_loc + bc_loc + heads_loc
    run_order = jnp.arange(run_count, dtype=jnp.int32)
    run_ends = jnp.cumsum(lengths, axis=1)
    start_flag = jnp.any((run_ends - lengths)[:, :, None] == run_order[None, None, :], axis=1)
    conv_taps = jnp.concatenate([conv_x, conv_bc], axis=1)
    conv_bias = jnp.concatenate([conv_x_bias, conv_bc_bias])
    neg_rate = -jnp.exp(a_log)
    lower_tri = jnp.arange(BLOCK)[:, None] >= jnp.arange(BLOCK)[None, :]
    tri_f = lower_tri.astype(jnp.float32)
    head_zero = jnp.zeros((heads_loc,), jnp.float32)
    state_zero = jnp.zeros((heads_loc, HDIM, STATE), jnp.float32)
    grad_shard = jnp.zeros((own_rows, width_in + inner_loc), jnp.float32)
    g_conv = jnp.zeros_like(conv_taps)
    g_conv_bias = jnp.zeros_like(conv_bias)
    g_dt_bias = head_zero
    g_a_log = head_zero
    g_skip = head_zero
    norm_gain_gradient = jnp.zeros((portion_length,), jnp.float32)
    g_gate = jnp.zeros((inner_loc,), jnp.float32)
    out_rows = []
    grad_rows = []
    for micro_at in range(micro_count):
        row_owner = dealing[micro_at]
        seq_flags = start_flag[micro_at]
        run_pos = jnp.sum(jnp.where(row_owner == seq_at, run_order, 0))
        keep_in = 1.0 - seq_flags[run_pos].astype(jnp.float32)
        seq_first = jnp.max(jnp.where(seq_flags & (run_order <= run_pos), run_order, 0))
        next_start = jnp.min(jnp.where(seq_flags & (run_order > run_pos), run_order, run_count))
        pred_dev = row_owner[jnp.maximum(run_pos - 1, 0)]
        succ_dev = row_owner[jnp.minimum(run_pos + 1, run_count - 1)]
        has_next = (run_pos + 1 < run_count).astype(jnp.float32)
        row_lo = micro_at * run_len
        hidden_f = hidden[row_lo : row_lo + run_len].astype(jnp.float32)
        reciprocal_root_mean = lax.rsqrt(jnp.mean(hidden_f * hidden_f, axis=1) + EPSILON)
        normalized_input = hidden_f * reciprocal_root_mean[:, None]
        normed = (normalized_input * norm_gain).astype(jnp.bfloat16)
        weights = (
            lax.all_gather(z_proj, "seq", axis=0, tiled=True),
            lax.all_gather(x_proj, "seq", axis=0, tiled=True),
            lax.all_gather(bc_proj, "seq", axis=0, tiled=True),
            lax.all_gather(dt_proj, "seq", axis=0, tiled=True),
            lax.all_gather(out_proj, "seq", axis=0, tiled=True),
        )
        w_in = jnp.concatenate([weights[0], weights[1], weights[2], weights[3]], axis=1)
        w_out = weights[4]
        projected = jnp.dot(normed, w_in, preferred_element_type=jnp.float32)
        gate_low = projected[:, :inner_loc].astype(jnp.bfloat16)
        conv_in = projected[:, inner_loc : 2 * inner_loc + bc_loc].astype(jnp.bfloat16)
        dt_in = projected[:, 2 * inner_loc + bc_loc :]
        edge_rows = lax.all_gather(conv_in[run_len - 3 :], "seq", axis=0, tiled=True)
        edge_prev = (
            lax.dynamic_slice_in_dim(edge_rows, pred_dev * 3, 3, 0).astype(jnp.float32) * keep_in
        )
        extended = jnp.concatenate([edge_prev, conv_in.astype(jnp.float32)], axis=0)
        conv_pre = conv_bias
        for tap_at in range(4):
            conv_pre = conv_pre + conv_taps[tap_at] * extended[tap_at : tap_at + run_len]
        conv_act = jax.nn.silu(conv_pre)
        x_mix = conv_act[:, :inner_loc].astype(jnp.bfloat16)
        bc_all = lax.all_gather(
            conv_act[:, inner_loc:].astype(jnp.bfloat16), "head", axis=1, tiled=True
        )
        b_mat = bc_all[:, :STATE]
        c_mat = bc_all[:, STATE:]
        dt_val = jax.nn.softplus(dt_in + dt_bias)
        rate_val = dt_val * neg_rate
        x_heads = x_mix.reshape(run_len, heads_loc, HDIM).transpose(1, 0, 2)
        entry_zero = state_zero
        x_part = x_heads
        b_part = b_mat
        c_part = c_mat
        dt_part = dt_val.T
        cum_rate = jnp.cumsum(rate_val.T, axis=1)
        lam_part = cum_rate[:, -1]
        w_end = jnp.exp(lam_part[:, None] - cum_rate) * dt_part
        s_part = mixed_einsum("hqp,qn->hpn", w_end[:, :, None] * x_part.astype(jnp.float32), b_part)
        stored = [(x_part, b_part, c_part, dt_part, cum_rate, lam_part, w_end, entry_zero)]
        entry_zero = jnp.exp(lam_part)[:, None, None] * entry_zero + s_part
        lam_run = lam_part
        run_states, run_rates = (
            lax.all_gather(entry_zero[None].astype(jnp.bfloat16), "seq", axis=0, tiled=True).astype(
                jnp.float32
            ),
            lax.all_gather(lam_run[None].astype(jnp.bfloat16), "seq", axis=0, tiled=True).astype(
                jnp.float32
            ),
        )
        state_ord = run_states[row_owner]
        rate_ord = run_rates[row_owner]
        before_me = (
            (run_order[:, None] < run_order[None, :]) & (run_order[None, :] < run_pos)
        ).astype(jnp.float32)
        valid_in = ((run_order >= seq_first) & (run_order < run_pos)).astype(jnp.float32)
        coef_in = jnp.exp(jnp.dot(before_me, rate_ord, precision=HIGHEST)) * valid_in[:, None]
        state_in = jnp.einsum("qh,qhan->han", coef_in, state_ord, precision=HIGHEST)
        prefix = head_zero
        part_at = 0
        x_part, b_part, c_part, dt_part, cum_rate, lam_part, w_end, entry_part = stored[part_at]
        exp_prefix = jnp.exp(prefix)
        entry_true = entry_part + exp_prefix[:, None, None] * state_in
        scores = contract_cols(c_part, b_part)
        exponent = jnp.where(lower_tri[None], cum_rate[:, :, None] - cum_rate[:, None, :], 0.0)
        decay_mask = jnp.exp(exponent) * tri_f[None]
        mix_wt = (scores[None] * decay_mask * dt_part[:, None, :]).astype(jnp.bfloat16)
        inner_out = jnp.einsum("hij,hjp->hip", mix_wt, x_part, preferred_element_type=jnp.float32)
        outer_out = jnp.exp(cum_rate)[:, :, None] * mixed_einsum("in,hpn->hip", c_part, entry_true)
        ssd_parts = [inner_out + outer_out + d_skip[:, None, None] * x_part.astype(jnp.float32)]
        kept_fwd = [(scores, decay_mask, mix_wt, outer_out, entry_true, exp_prefix)]
        prefix = lam_part
        ssd_out = jnp.concatenate(ssd_parts, axis=1).transpose(1, 0, 2).reshape(run_len, inner_loc)
        gate_f = gate_low.astype(jnp.float32)
        gate_act = jax.nn.silu(gate_f)
        gated = ssd_out * gate_act
        gate_total = lax.psum(jnp.sum(gated * gated, axis=1), "head")
        inv_gate = lax.rsqrt(gate_total / INNER + EPSILON)
        scaled = gated * inv_gate[:, None]
        branch = (scaled * gate_gain).astype(jnp.bfloat16)
        partial_out = contract_cols(branch, w_out)
        out_piece = lax.psum_scatter(
            partial_out.astype(jnp.bfloat16), "head", scatter_dimension=1, tiled=True
        ).astype(jnp.float32)
        hidden_share = lax.dynamic_slice_in_dim(
            hidden_f, head_offset * portion_length, portion_length, 1
        )
        out_rows.append((hidden_share + out_piece).astype(jnp.bfloat16))
        cot_rows = cotangent[row_lo : row_lo + run_len]
        d_branch = jnp.dot(cot_rows, w_out, preferred_element_type=jnp.float32)
        d_scaled = d_branch * gate_gain
        g_gate = g_gate + jnp.sum(d_branch * scaled, axis=0)
        back_stat = lax.psum(jnp.sum(d_scaled * scaled, axis=1), "head")
        d_gated = inv_gate[:, None] * (d_scaled - scaled * (back_stat / INNER)[:, None])
        d_ssd = (d_gated * gate_act).astype(jnp.bfloat16)
        d_gate = d_gated * ssd_out * silu_grad(gate_f)
        dy_heads = d_ssd.reshape(run_len, heads_loc, HDIM).transpose(1, 0, 2)
        part_at = 0
        c_part = stored[part_at][2]
        cum_rate = stored[part_at][4]
        exp_prefix = kept_fwd[part_at][5]
        dy_f = dy_heads.astype(jnp.float32)
        d_entry = mixed_einsum("hip,in->hpn", dy_f * jnp.exp(cum_rate)[:, :, None], c_part)
        d_entries = [d_entry]
        grad_in = exp_prefix[:, None, None] * d_entry
        pref_gain = [exp_prefix * jnp.sum(d_entry * state_in, axis=(1, 2))]
        grads_all = lax.all_gather(
            grad_in[None].astype(jnp.bfloat16), "seq", axis=0, tiled=True
        ).astype(jnp.float32)
        grad_ord = grads_all[row_owner]
        after_me = (
            (run_pos < run_order[None, :]) & (run_order[None, :] < run_order[:, None])
        ).astype(jnp.float32)
        valid_out = ((run_order > run_pos) & (run_order < next_start)).astype(jnp.float32)
        coef_out = jnp.exp(jnp.dot(after_me, rate_ord, precision=HIGHEST)) * valid_out[:, None]
        d_state = jnp.einsum("ph,phan->han", coef_out, grad_ord, precision=HIGHEST)
        d_lam_run = jnp.exp(lam_run) * jnp.sum(d_state * state_in, axis=(1, 2))
        d_next = d_state
        running = head_zero
        block_grads = [None] * n_blocks
        for part_at in reversed(range(n_blocks)):
            x_part, b_part, c_part, dt_part, cum_rate, lam_part, w_end, entry_part = stored[part_at]
            scores, decay_mask, mix_wt, outer_out, entry_true, exp_prefix = kept_fwd[part_at]
            d_send = d_next
            lam_grad = (
                d_lam_run + running + jnp.exp(lam_part) * jnp.sum(d_next * entry_part, axis=(1, 2))
            )
            running = running + pref_gain[part_at]
            d_next = d_entries[part_at] + jnp.exp(lam_part)[:, None, None] * d_next
            x_f = x_part.astype(jnp.float32)
            dy_f = dy_heads.astype(jnp.float32)
            dc_part = mixed_einsum("hip,hpn->in", dy_f * jnp.exp(cum_rate)[:, :, None], entry_true)
            d_cum = jnp.sum(dy_f * outer_out, axis=2)
            along_b = mixed_einsum("hpn,qn->hqp", d_send, b_part)
            d_wend = jnp.sum(along_b * x_f, axis=2)
            dx_part = w_end[:, :, None] * along_b
            db_part = mixed_einsum("hqp,hpn->qn", w_end[:, :, None] * x_f, d_send)
            end_gain = d_wend * w_end
            d_dt = d_wend * jnp.exp(lam_part[:, None] - cum_rate)
            d_cum = d_cum - end_gain
            d_cum = d_cum.at[:, -1].add(lam_grad + jnp.sum(end_gain, axis=1))
            d_mix = jnp.einsum("hip,hjp->hij", dy_heads, x_part, preferred_element_type=jnp.float32)
            dx_part = dx_part + jnp.einsum(
                "hij,hip->hjp", mix_wt, dy_heads, preferred_element_type=jnp.float32
            )
            masked = d_mix * decay_mask
            d_scores = jnp.sum(masked * dt_part[:, None, :], axis=0).astype(jnp.bfloat16)
            d_dt = d_dt + jnp.sum(masked * scores[None], axis=1)
            d_expo = masked * scores[None] * dt_part[:, None, :]
            d_cum = d_cum + jnp.sum(d_expo, axis=2) - jnp.sum(d_expo, axis=1)
            dc_part = dc_part + jnp.dot(d_scores, b_part, preferred_element_type=jnp.float32)
            db_part = db_part + contract_rows(d_scores, c_part)
            g_skip = g_skip + jnp.sum(dy_f * x_f, axis=(1, 2))
            dx_part = dx_part + d_skip[:, None, None] * dy_f
            d_rate = lax.cumsum(d_cum, axis=1, reverse=True)
            block_grads[part_at] = (dx_part, db_part, dc_part, d_dt, d_rate)
        dx_flat = (
            jnp.concatenate([item[0] for item in block_grads], axis=1)
            .transpose(1, 0, 2)
            .reshape(run_len, inner_loc)
        )
        db_all = jnp.concatenate([item[1] for item in block_grads], axis=0)
        dc_all = jnp.concatenate([item[2] for item in block_grads], axis=0)
        d_dt_all = jnp.concatenate([item[3] for item in block_grads], axis=1).T
        d_rate_all = jnp.concatenate([item[4] for item in block_grads], axis=1).T
        g_a_log = g_a_log + jnp.sum(d_rate_all * dt_val, axis=0) * neg_rate
        d_dt_in = (d_dt_all + d_rate_all * neg_rate) * jax.nn.sigmoid(dt_in + dt_bias)
        g_dt_bias = g_dt_bias + jnp.sum(d_dt_in, axis=0)
        d_bc = lax.psum_scatter(
            jnp.concatenate([db_all, dc_all], axis=1).astype(jnp.bfloat16),
            "head",
            scatter_dimension=1,
            tiled=True,
        ).astype(jnp.float32)
        d_conv = jnp.concatenate([dx_flat, d_bc], axis=1) * silu_grad(conv_pre)
        g_conv_bias = g_conv_bias + jnp.sum(d_conv, axis=0)
        g_conv = g_conv + jnp.stack(
            [jnp.sum(d_conv * extended[tap_at : tap_at + run_len], axis=0) for tap_at in range(4)]
        )
        d_ext = jnp.zeros((run_len + 3, conv_taps.shape[1]), jnp.float32)
        for tap_at in range(4):
            d_ext = d_ext + jnp.pad(conv_taps[tap_at] * d_conv, ((tap_at, 3 - tap_at), (0, 0)))
        back_edges = lax.all_gather(d_ext[:3] * keep_in, "seq", axis=0, tiled=True)
        incoming = lax.dynamic_slice_in_dim(back_edges, succ_dev * 3, 3, 0) * has_next
        d_conv_in = d_ext[3:] + jnp.pad(incoming, ((run_len - 3, 0), (0, 0)))
        d_proj = jnp.concatenate(
            [
                d_gate.astype(jnp.bfloat16),
                d_conv_in.astype(jnp.bfloat16),
                d_dt_in.astype(jnp.bfloat16),
            ],
            axis=1,
        )
        d_normed = contract_cols(d_proj, w_in)
        gradient_portion = lax.psum_scatter(
            d_normed.astype(jnp.bfloat16), "head", scatter_dimension=1, tiled=True
        ).astype(jnp.float32)
        normalized_portion = lax.dynamic_slice_in_dim(
            normalized_input, head_offset * portion_length, portion_length, 1
        )
        gain_portion = lax.dynamic_slice_in_dim(
            norm_gain, head_offset * portion_length, portion_length, 0
        )
        normalized_gradient = gradient_portion * gain_portion
        norm_gain_gradient = norm_gain_gradient + jnp.sum(
            gradient_portion * normalized_portion, axis=0
        )
        row_statistic = lax.psum(jnp.sum(normalized_gradient * normalized_portion, axis=1), "head")
        cotangent_portion = lax.dynamic_slice_in_dim(
            cot_rows, head_offset * portion_length, portion_length, 1
        ).astype(jnp.float32)
        grad_rows.append(
            reciprocal_root_mean[:, None]
            * (normalized_gradient - normalized_portion * (row_statistic / MODEL_WIDTH)[:, None])
            + cotangent_portion
        )

        def grad_term(
            row_start, row_count, normed=normed, d_proj=d_proj, cot_rows=cot_rows, branch=branch
        ):
            return jnp.concatenate(
                [contract_rows(normed, d_proj), contract_rows(cot_rows, branch)], axis=1
            )

        grad_shard = grad_shard + scatter_rows(grad_term, own_rows)
    summed = lax.psum(
        (g_conv, g_conv_bias, g_dt_bias, g_a_log, g_skip, norm_gain_gradient, g_gate), "seq"
    )
    conv_sum, conv_bias_sum, dt_bias_sum, a_log_sum, skip_sum, norm_sum, gate_sum = summed
    cut_two = 2 * inner_loc
    cut_three = cut_two + bc_loc
    cut_four = cut_three + heads_loc
    return (
        jnp.concatenate(out_rows, axis=0),
        jnp.concatenate(grad_rows, axis=0),
        grad_shard[:, :inner_loc],
        grad_shard[:, inner_loc:cut_two],
        grad_shard[:, cut_two:cut_three],
        grad_shard[:, cut_three:cut_four],
        grad_shard[:, cut_four:],
        conv_sum[:, :inner_loc],
        conv_bias_sum[:inner_loc],
        conv_sum[:, inner_loc:],
        conv_bias_sum[inner_loc:],
        dt_bias_sum,
        a_log_sum,
        skip_sum,
        norm_sum,
        gate_sum,
    )


def solution(mesh):
    return jax.shard_map(
        per_device,
        mesh=mesh,
        in_specs=(
            P("seq", None),
            P("seq", None),
            P("seq", "head"),
            P("seq", "head"),
            P("seq", "head"),
            P("seq", "head"),
            P("seq", "head"),
            P(None, "head"),
            P("head"),
            P(None, "head"),
            P("head"),
            P("head"),
            P("head"),
            P("head"),
            P(),
            P("head"),
            P(),
            P(),
        ),
        out_specs=(
            P("seq", "head"),
            P("seq", "head"),
            P("seq", "head"),
            P("seq", "head"),
            P("seq", "head"),
            P("seq", "head"),
            P("seq", "head"),
            P(None, "head"),
            P("head"),
            P(None, "head"),
            P("head"),
            P("head"),
            P("head"),
            P("head"),
            P("head"),
            P("head"),
        ),
        check_vma=False,
    )
```

profile of v0, /device:TPU:0, one launch (start us, length us, event | category | flops | bytes accessed | tf_op | source)
XLA Modules:
  0.0 1486.0 jit_solution(2980562678117627075)
XLA Ops:
  18.8 43.6 %all-gather.6 = bf16[16,96,24]{1,2,0:T(8,128)(2,1)S(1)} all-gather(bf16[1,96,24]{1,2,0:T(8,128)(2,1)} %bitcast.430), channel_id=1, replica_groups=mesh['seq'=16,'head'=2] {'seq'}, dimensions={0}, use_global_device_ids=true | all-gather | bytes 78336 | tf_op jit(solution)/shard_map/all_gather | solution.py:141
  63.4 43.0 %all_gather.58 = bf16[1536,128]{1,0:T(8,128)(2,1)} all-gather(bf16[96,128]{1,0:T(8,128)(2,1)} %param.26), channel_id=1, replica_groups=mesh['seq'=16,'head'=2] {'seq'}, dimensions={0}, use_global_device_ids=true | all-gather | bytes 417792 | tf_op jit(solution)/shard_map/all_gather | solution.py:140
  110.6 71.1 %all-gather.19.cloned.1.call-done = bf16[1536,1536]{1,0:T(8,128)(2,1)} async-done(((bf16[96,1536]{1,0:T(8,128)(2,1)}), bf16[1536,1536]{1,0:T(8,128)(2,1)}) %all-gather.19.cloned.1.call-update) | async-done | bytes 4718608 | tf_op jit(solution)/shard_map/all_gather | solution.py:138
  181.8 9.9 fusion.257
  193.9 40.1 %all-gather.7 = bf16[16,3,1664]{2,1,0:T(4,128)(2,1)S(1)} all-gather(bf16[1,3,1664]{2,1,0:T(4,128)(2,1)S(1)} %copy.274), channel_id=1, replica_groups=mesh['seq'=16,'head'=2] {'seq'}, dimensions={0}, use_global_device_ids=true | all-gather | bytes 169728 | tf_op jit(solution)/shard_map/all_gather | solution.py:150
  236.7 9.9 fusion.256
  248.2 37.3 %all-gather.8 = bf16[16,3,1664]{2,1,0:T(4,128)(2,1)S(1)} all-gather(bf16[1,3,1664]{2,1,0:T(4,128)(2,1)S(1)} %copy.288), channel_id=1, replica_groups=mesh['seq'=16,'head'=2] {'seq'}, dimensions={0}, use_global_device_ids=true | all-gather | bytes 169728 | tf_op jit(solution)/shard_map/all_gather | solution.py:150
  288.3 6.2 multiply_convert_fusion.7
  312.8 2.6 and_convert_fusion.2
  318.0 39.7 %all-reduce.16 = (bf16[384]{0:T(512)(128)(2,1)S(1)}, bf16[384]{0:T(512)(128)(2,1)S(1)}) all-reduce(bf16[384]{0:T(512)(128)(2,1)S(1)} %dynamic-update-slice.7, bf16[384]{0:T(512)(128)(2,1)S(1)} %dynamic-update-slice.6), channel_id=4, replica_groups=mesh['seq'=16,'head'=2] {'seq'}, use_global_device_ids=true, to_apply=%add.11 | all-reduce | flops 768 | bytes 3072
  365.4 5.7 fusion.241
  371.2 24.0 %all-gather.27.cloned.1.call-done = bf16[384,64,128]{2,1,0:T(8,128)(2,1)} async-done(((bf16[24,64,128]{2,1,0:T(8,128)(2,1)}), bf16[384,64,128]{2,1,0:T(8,128)(2,1)}) %all-gather.27.cloned.1.call-update) | async-done | bytes 6291472 | tf_op jit(solution)/shard_map/all_gather | solution.py:181
  395.1 6.7 gather_fusion.3
  401.9 9.0 fusion.6
  415.4 3.4 multiply_reduce_fusion.20
  418.8 72.1 %all-gather.25.cloned.1.call-done = bf16[384,64,128]{2,1,0:T(8,128)(2,1)} async-done(((bf16[24,64,128]{2,1,0:T(8,128)(2,1)}), bf16[384,64,128]{2,1,0:T(8,128)(2,1)}) %all-gather.25.cloned.1.call-update) | async-done | bytes 6291472 | tf_op jit(solution)/shard_map/all_gather | solution.py:181
  490.8 6.9 gather_fusion.1
  497.8 9.1 fusion.8
  510.2 2.8 multiply_reduce_fusion.22
  513.0 3.1 all-reduce.15
  517.5 7.5 multiply_reduce_fusion.17
  525.0 3.1 all-reduce.14
  529.6 6.1 fusion.41
  543.8 3.1 and_convert_fusion
  555.6 5.1 multiply_reduce_fusion.3
  562.0 5.1 multiply_reduce_fusion.5
  567.9 62.4 %all-gather.31.cloned.1.call-done = bf16[384,64,128]{2,1,0:T(8,128)(2,1)} async-done(((bf16[24,64,128]{2,1,0:T(8,128)(2,1)}), bf16[384,64,128]{2,1,0:T(8,128)(2,1)}) %all-gather.31.cloned.1.call-update) | async-done | bytes 6291472 | tf_op jit(solution)/shard_map/all_gather | solution.py:244
  630.3 6.8 gather_fusion.5
  637.1 9.1 fusion.2
  648.3 77.8 %all-gather.29.cloned.1.call-done = bf16[384,64,128]{2,1,0:T(8,128)(2,1)} async-done(((bf16[24,64,128]{2,1,0:T(8,128)(2,1)}), bf16[384,64,128]{2,1,0:T(8,128)(2,1)}) %all-gather.29.cloned.1.call-update) | async-done | bytes 6291472 | tf_op jit(solution)/shard_map/all_gather | solution.py:244
  726.1 6.9 gather_fusion.4
  733.0 9.4 fusion.4
  748.3 5.5 convolution_convert_fusion.6
  767.3 5.4 fusion.1
  772.7 5.1 convolution_convert_fusion.7
  781.5 2.5 fusion.53
  788.6 2.7 reduce-window.36
  792.3 4.4 fusion.51
  797.2 2.5 reduce-window.34
  803.4 5.0 fusion.54
  808.4 3.2 fusion.55
  812.5 7.0 fusion.246
  820.4 7.1 fusion.247
  827.5 3.1 broadcast_multiply_fusion.6
  830.6 3.5 pad_add_fusion.1
  836.9 42.7 %all-gather.9 = f32[16,3,1664]{2,1,0:T(4,128)} all-gather(f32[1,3,1664]{2,1,0:T(4,128)S(1)} %copy.309), channel_id=1, replica_groups=mesh['seq'=16,'head'=2] {'seq'}, dimensions={0}, use_global_device_ids=true | all-gather | bytes 339456 | tf_op jit(solution)/shard_map/all_gather | solution.py:320
  883.5 2.8 fusion.90
  887.8 40.1 %all-gather.10 = f32[16,3,1664]{2,1,0:T(4,128)} all-gather(f32[1,3,1664]{2,1,0:T(4,128)S(1)} %copy.328), channel_id=1, replica_groups=mesh['seq'=16,'head'=2] {'seq'}, dimensions={0}, use_global_device_ids=true | all-gather | bytes 339456 | tf_op jit(solution)/shard_map/all_gather | solution.py:320
  931.0 3.2 fusion.29
  936.4 5.6 pad_add_fusion
  942.0 6.4 convolution_convert_fusion.5
  948.6 2.5 fusion.28
  951.2 9.4 convolution_convert_fusion
  960.6 6.1 convolution_convert_fusion.4
  966.8 16.8 %pad_maximum_fusion.1 = bf16[1536,4760]{0,1:T(8,128)(2,1)} fusion(bf16[1536,1536]{0,1:T(8,128)(2,1)} %fusion.1, bf16[1536,3224]{0,1:T(8,128)(2,1)} %convolution_convert_fusion), kind=kLoop, calls=%fused_computation.9 | loop fusion | flops 29245440 | bytes 29245440 | tf_op jit(solution)/shard_map/concatenate | solution.py:358
  983.6 18.7 %copy.395 = bf16[1536,4760]{1,0:T(8,128)(2,1)} copy(bf16[1536,4760]{0,1:T(8,128)(2,1)} %pad_maximum_fusion.1) | data formatting | bytes 29245440
  1003.7 4.7 fusion
  1008.4 4.4 convolution_convert_fusion.1
  1012.9 18.3 %pad_maximum_fusion = bf16[1536,4760]{0,1:T(8,128)(2,1)} fusion(bf16[1536,1536]{0,1:T(8,128)(2,1)S(1)} %copy-done.3, bf16[1536,3224]{0,1:T(8,128)(2,1)S(1)} %convolution_convert_fusion.1), kind=kLoop, calls=%fused_computation.8 | loop fusion | flops 29245440 | bytes 29245440 | tf_op jit(solution)/shard_map/concatenate | solution.py:358
  1031.2 20.1 %copy.393 = bf16[1536,4760]{1,0:T(8,128)(2,1)} copy(bf16[1536,4760]{0,1:T(8,128)(2,1)} %pad_maximum_fusion) | data formatting | bytes 29245440
  1067.2 75.5 %all-reduce.12 = (f32[4,1664]{1,0:T(4,128)}, f32[1664]{0:T(1024)}, f32[24]{0:T(128)}, f32[24]{0:T(128)}, f32[24]{0:T(128)}, /*index=5*/f32[768]{0:T(1024)}, f32[1536]{0:T(1024)}) all-reduce(f32[4,1664]{1,0:T(4,128)} %maximum_add_fusion, f32[1664]{0:T(1024)} %add.574, f32[24]{0:T(128)} %add.575, ...), channel_id=1, replica_groups=mesh['seq'=16,'head'=2] {'seq'}, use_global_device_ids=true, to_apply=%region_64.65 | all-reduce | flops 10696 | bytes 85568 | tf_op jit(solution)/shard_map/psum | solution.py:363
  1146.5 3.1 all-reduce.13
  1153.2 79.0 %reduce-scatter.27.cloned.1.call-done = bf16[96,4760]{1,0:T(8,128)(2,1)} async-done(((bf16[1536,4760]{1,0:T(8,128)(2,1)}), bf16[96,4760]{1,0:T(8,128)(2,1)}) %reduce-scatter.27.cloned.1.call-update) | async-done | bytes 913936
  1234.5 232.8 %reduce-scatter.25.cloned.1.call-done = bf16[96,4760]{1,0:T(8,128)(2,1)} async-done(((bf16[1536,4760]{1,0:T(8,128)(2,1)}), bf16[96,4760]{1,0:T(8,128)(2,1)}) %reduce-scatter.25.cloned.1.call-update) | async-done | bytes 913936
  (623 shorter events, 160.7 us)
Async XLA Ops:
  7.2 99.2 %copy-start.4 = (bf16[512,1536]{1,0:T(8,128)(2,1)S(1)}, bf16[512,1536]{1,0:T(8,128)(2,1)}, u32[]{:S(2)}) copy-start(bf16[512,1536]{1,0:T(8,128)(2,1)} %param.22) | copy-start | bytes 4718596
  7.2 103.4 %all-gather.21.cloned.1.call-start = ((), (), s32[]{:S(2)}) async-start(), calls=%async_computation.9 | async-start | bytes 5013504 | tf_op jit(solution)/shard_map/all_gather | solution.py:139
  7.9 98.9 %copy-start.147 = (f32[4,1536]{1,0:T(4,128)S(1)}, f32[4,1536]{1,0:T(4,128)}, u32[]{:S(2)}) copy-start(f32[4,1536]{1,0:T(4,128)} %param.29) | copy-start | bytes 73732
  7.9 98.9 %copy-start.163 = (f32[4,128]{1,0:T(4,128)S(1)}, f32[4,128]{1,0:T(4,128)}, u32[]{:S(2)}) copy-start(f32[4,128]{1,0:T(4,128)} %param.31) | copy-start | bytes 6148
  7.9 99.0 %copy-start.156 = (s32[2,8]{1,0:T(2,128)S(1)}, s32[2,8]{1,0:T(2,128)}, u32[]{:S(2)}) copy-start(s32[2,8]{1,0:T(2,128)} %param.38) | copy-start | bytes 196
  8.0 102.5 %copy-start.171 = (f32[24]{0:T(128)S(1)}, f32[24]{0:T(128)}, u32[]{:S(2)}) copy-start(f32[24]{0:T(128)} %param.34) | copy-start | bytes 292
  8.0 102.6 %copy-start.149 = (f32[1536]{0:T(1024)S(1)}, f32[1536]{0:T(1024)}, u32[]{:S(2)}) copy-start(f32[1536]{0:T(1024)} %param.30) | copy-start | bytes 18436
  8.0 102.6 %copy-start.170 = (f32[128]{0:T(128)S(1)}, f32[128]{0:T(128)}, u32[]{:S(2)}) copy-start(f32[128]{0:T(128)} %param.32) | copy-start | bytes 1540
  8.0 173.8 %copy-start.82 = (f32[1536]{0:T(1024)S(1)}, f32[1536]{0:T(1024)}, u32[]{:S(2)}) copy-start(f32[1536]{0:T(1024)} %param.36) | copy-start | bytes 18436
  8.0 173.8 %all-gather.19.cloned.1.call-start = ((), (), s32[]{:S(2)}) async-start(), calls=%async_computation.8 | async-start | bytes 5013504 | tf_op jit(solution)/shard_map/all_gather | solution.py:138
  8.7 356.7 %all-gather.23.cloned.1.call-start = ((), (), s32[]{:S(2)}) async-start(), calls=%async_computation.10 | async-start | bytes 5013504 | tf_op jit(solution)/shard_map/all_gather | solution.py:142
  9.5 385.7 %all-gather.27.cloned.1.call-start = ((), (), s32[]{:S(2)}) async-start(), calls=%async_computation.18 | async-start | bytes 6684672 | tf_op jit(solution)/shard_map/all_gather | solution.py:181
  106.9 181.3 %copy-start.95 = (f32[1664]{0:T(1024)}, f32[1664]{0:T(1024)S(1)}, u32[]{:S(2)}) copy-start(f32[1664]{0:T(1024)S(1)} %get-tuple-element.180) | copy-start | bytes 19972
  106.9 181.3 %copy-start.97 = (f32[1664]{0:T(1024)}, f32[1664]{0:T(1024)S(1)}, u32[]{:S(2)}) copy-start(f32[1664]{0:T(1024)S(1)} %get-tuple-element.181) | copy-start | bytes 19972
  107.0 181.3 %copy-start.99 = (f32[1664]{0:T(1024)}, f32[1664]{0:T(1024)S(1)}, u32[]{:S(2)}) copy-start(f32[1664]{0:T(1024)S(1)} %get-tuple-element.182) | copy-start | bytes 19972
  107.0 181.3 %copy-start.101 = (f32[1664]{0:T(1024)}, f32[1664]{0:T(1024)S(1)}, u32[]{:S(2)}) copy-start(f32[1664]{0:T(1024)S(1)} %get-tuple-element.183) | copy-start | bytes 19972
  110.5 185.8 %copy-start.157 = (f32[24]{0:T(128)}, f32[24]{0:T(128)S(1)}, u32[]{:S(2)}) copy-start(f32[24]{0:T(128)S(1)} %exponential_negate_fusion) | copy-start | bytes 292
  110.5 81.1 %copy-start.113 = (f32[256]{0:T(256)}, f32[256]{0:T(256)S(1)}, u32[]{:S(2)}) copy-start(f32[256]{0:T(256)S(1)} %get-tuple-element.292) | copy-start | bytes 3076
  110.5 126.1 %copy-start.110 = (f32[256]{0:T(256)}, f32[256]{0:T(256)S(1)}, u32[]{:S(2)}) copy-start(f32[256]{0:T(256)S(1)} %get-tuple-element.291) | copy-start | bytes 3076
  191.6 94.5 %copy-start.27 = (bf16[256,3224]{0,1:T(8,128)(2,1)}, bf16[256,3224]{0,1:T(8,128)(2,1)S(1)}, u32[]{:S(2)}) copy-start(bf16[256,3224]{0,1:T(8,128)(2,1)S(1)} %get-tuple-element.286) | copy-start | bytes 4952068
  246.6 39.4 %copy-start.53 = (bf16[3,1664]{0,1:T(8,128)(2,1)S(1)}, bf16[3,1664]{0,1:T(8,128)(2,1)}, u32[]{:S(2)}) copy-start(bf16[3,1664]{0,1:T(8,128)(2,1)} %copy.398) | copy-start | bytes 29956
  294.6 117.0 %copy-start.12 = (bf16[256,1536]{0,1:T(8,128)(2,1)}, bf16[256,1536]{0,1:T(8,128)(2,1)S(1)}, u32[]{:S(2)}) copy-start(bf16[256,1536]{0,1:T(8,128)(2,1)S(1)} %slice.333) | copy-start | bytes 2359300
  296.3 8.0 copy-start.51
  302.5 188.3 %all-gather.25.cloned.1.call-start = ((), (), s32[]{:S(2)}) async-start(), calls=%async_computation.17 | async-start | bytes 6684672 | tf_op jit(solution)/shard_map/all_gather | solution.py:181
  303.3 204.3 %copy-start.17 = (bf16[256,1536]{0,1:T(8,128)(2,1)}, bf16[256,1536]{0,1:T(8,128)(2,1)S(1)}, u32[]{:S(2)}) copy-start(bf16[256,1536]{0,1:T(8,128)(2,1)S(1)} %slice.319) | copy-start | bytes 2359300
  304.3 13.5 copy-start.44
  304.5 59.8 %copy-start.56 = (f32[24,256]{0,1:T(8,128)}, f32[24,256]{0,1:T(8,128)S(1)}, u32[]{:S(2)}) copy-start(f32[24,256]{0,1:T(8,128)S(1)} %get-tuple-element.254) | copy-start | bytes 73732
  306.7 8.7 copy-start.148
  308.3 322.0 %all-gather.31.cloned.1.call-start = ((), (), s32[]{:S(2)}) async-start(), calls=%async_computation.20 | async-start | bytes 6684672 | tf_op jit(solution)/shard_map/all_gather | solution.py:244
  315.5 79.7 %copy-start.153 = (s32[1024]{0:T(1024)}, s32[1024]{0:T(1024)S(1)}, u32[]{:S(2)}) copy-start(s32[1024]{0:T(1024)S(1)} %pad_clamp_fusion) | copy-start | bytes 12292
  315.5 55.7 %copy-start.152 = (s32[1024]{0:T(1024)}, s32[1024]{0:T(1024)S(1)}, u32[]{:S(2)}) copy-start(s32[1024]{0:T(1024)S(1)} %pad_clamp_fusion.1) | copy-start | bytes 12292
  316.2 191.4 %copy-start.83 = (f32[256,256]{1,0:T(8,128)}, f32[256,256]{1,0:T(8,128)S(1)}, u32[]{:S(2)}) copy-start(f32[256,256]{1,0:T(8,128)S(1)} %get-tuple-element.306) | copy-start | bytes 786436
  358.4 12.8 copy-start.154
  362.8 8.4 copy-start.155
  365.2 46.5 %copy-start.89 = (f32[256,256]{1,0:T(8,128)}, f32[256,256]{1,0:T(8,128)S(1)}, u32[]{:S(2)}) copy-start(f32[256,256]{1,0:T(8,128)S(1)} %fusion.164) | copy-start | bytes 786436
  365.4 142.2 %copy-start.86 = (f32[256,256]{1,0:T(8,128)}, f32[256,256]{1,0:T(8,128)S(1)}, u32[]{:S(2)}) copy-start(f32[256,256]{1,0:T(8,128)S(1)} %fusion.177) | copy-start | bytes 786436
  513.0 16.5 %copy-start = (f32[256,1536]{0,1:T(8,128)}, f32[256,1536]{0,1:T(8,128)S(1)}, u32[]{:S(2)}) copy-start(f32[256,1536]{0,1:T(8,128)S(1)} %get-tuple-element.214) | copy-start | bytes 4718596
  516.8 8.2 copy-start.131
  517.5 7.5 copy-start.128
  537.7 188.4 %all-gather.29.cloned.1.call-start = ((), (), s32[]{:S(2)}) async-start(), calls=%async_computation.19 | async-start | bytes 6684672 | tf_op jit(solution)/shard_map/all_gather | solution.py:244
  539.9 12.5 copy-start.9
  541.9 269.8 %reduce-scatter.21.cloned.1.call-start = ((), (), s32[]{:S(2)}) async-start(), calls=%async_computation.15 | async-start | bytes 196608 | tf_op jit(solution)/shard_map/reduce_scatter | solution.py:306
  567.1 63.2 %copy-start.69 = (bf16[256,256]{1,0:T(8,128)(2,1)}, bf16[256,256]{1,0:T(8,128)(2,1)S(1)}, u32[]{:S(2)}) copy-start(bf16[256,256]{1,0:T(8,128)(2,1)S(1)} %get-tuple-element.143) | copy-start | bytes 393220
  637.1 9.1 copy-start.14
  637.1 9.1 copy-start.64
  732.9 9.4 copy-start.19
  733.0 9.4 copy-start.67
  745.7 73.8 %reduce-scatter.17.cloned.1.call-start = ((), (), s32[]{:S(2)}) async-start(), calls=%async_computation.13 | async-start | bytes 196608 | tf_op jit(solution)/shard_map/reduce_scatter | solution.py:306
  748.2 309.8 %reduce-scatter.15.cloned.1.call-start = ((), (), s32[]{:S(2)}) async-start(), calls=%async_computation.12 | async-start | bytes 1179648 | tf_op jit(solution)/shard_map/reduce_scatter | solution.py:219
  753.8 305.6 %reduce-scatter.13.cloned.1.call-start = ((), (), s32[]{:S(2)}) async-start(), calls=%async_computation.11 | async-start | bytes 1179648 | tf_op jit(solution)/shard_map/reduce_scatter | solution.py:219
  777.9 287.1 %reduce-scatter.19.cloned.1.call-start = ((), (), s32[]{:S(2)}) async-start(), calls=%async_computation.14 | async-start | bytes 1179648 | tf_op jit(solution)/shard_map/reduce_scatter | solution.py:332
  784.0 8.2 copy-start.7
  784.0 8.2 copy-start.20
  784.0 8.2 copy-start.62
  812.5 7.8 copy-start.22
  948.4 12.1 slice-start.1
  948.4 116.6 %reduce-scatter.23.cloned.1.call-start = ((), (), s32[]{:S(2)}) async-start(), calls=%async_computation.16 | async-start | bytes 1179648 | tf_op jit(solution)/shard_map/reduce_scatter | solution.py:332
  951.2 9.4 copy-start.79
  951.2 9.4 copy-start.81
  951.2 9.4 slice-start.2
  966.7 265.4 %reduce-scatter.27.cloned.1.call-start = ((), (), s32[]{:S(2)}) async-start(), calls=%async_computation.22 | async-start | bytes 15876096
  1002.4 464.9 %reduce-scatter.25.cloned.1.call-start = ((), (), s32[]{:S(2)}) async-start(), calls=%async_computation.21 | async-start | bytes 15876096
  1062.0 88.3 %copy-start.115 = (f32[256]{0:T(256)S(1)}, f32[256]{0:T(256)}, u32[]{:S(2)}) copy-start(f32[256]{0:T(256)} %copy-done.113) | copy-start | bytes 3076
  1065.0 85.3 %copy-start.55 = (bf16[256,768]{1,0:T(8,128)(2,1)S(1)}, bf16[256,768]{1,0:T(8,128)(2,1)}, u32[]{:S(2)}) copy-start(bf16[256,768]{1,0:T(8,128)(2,1)} %reduce-scatter.19.cloned.1.call-done) | copy-start | bytes 1179652
  (130 other events, 437.5 us)
Sparse Core Ops, SparseCore 0:
  10.8 88.0 all-gather.20
  101.7 79.9 all-gather.18
  184.6 84.0 all-gather.22
  302.7 92.4 all-gather.26
  398.3 92.4 all-gather.24
  537.8 92.4 all-gather.30
  633.6 92.4 all-gather.28
  745.9 5.7 reduce-scatter.20
  753.9 8.6 reduce-scatter.16
  765.3 9.4 reduce-scatter.14
  778.0 8.5 reduce-scatter.12
  948.6 6.4 reduce-scatter.18
  966.9 6.4 reduce-scatter.22
  1002.5 229.6 reduce-scatter.26
  1237.9 229.3 reduce-scatter.24
where the time goes:
time: 1500 us; the launch traced here: 1490 us
  waiting for transfers between devices  622 us (41%)
  blocking collectives  375 us (25%)
  matrix products  170 us (11%)
  local copies, waits for them, and re-layouts  147 us (10%)
  other arithmetic  144 us (10%)
  between operations  27.5 us (2%)
    unnamed x17, waiting for transfers between devices  314 us
    all_gather x2, waiting for transfers between devices, per_device(): lax.all_gather(grad_in[None].astype(jnp.bfloat16), 'seq', axis=0, tiled=T...  140 us
    all_gather x2, waiting for transfers between devices, per_device(): lax.all_gather(entry_zero[None].astype(jnp.bfloat16), 'seq', axis=0, tile...  96.1 us
    all_gather x2, blocking collectives, per_device(): back_edges = lax.all_gather(d_ext[:3] * keep_in, 'seq', axis=0, tiled=True)  82.8 us
    all_gather x2, blocking collectives, per_device(): edge_rows = lax.all_gather(conv_in[run_len - 3:], 'seq', axis=0, tiled=True)  77.4 us
    unnamed x389, local copies, waits for them, and re-layouts  76.2 us
    psum x1, blocking collectives, per_device(): lax.psum((g_conv, g_conv_bias, g_dt_bias, g_a_log, g_skip, norm_gain_grad...  75.5 us
    all_gather x1, waiting for transfers between devices, per_device(): lax.all_gather(z_proj, 'seq', axis=0, tiled=True)  71.1 us
  transfers between devices with their start and end apart: 15, of which 7 were waited for; matrix products, arithmetic and copies ran while one was open for 26% of the time, Pallas kernels for 0%

commit v1 on v0

v1 whole, which is shorter than its diff:
```python
import jax
import jax.numpy as jnp
from jax import lax
from jax.experimental import pallas as pl
from jax.experimental.pallas import tpu as pltpu
from jax.sharding import PartitionSpec as P

MODEL_WIDTH = 1536
HDIM = 64
STATE = 128
BLOCK = 256
INNER = 3072
HALO = 8
LANES = 128
EPSILON = 1e-05

F32 = jnp.float32
BF16 = jnp.bfloat16


def dot_nn(left, right):
    return lax.dot_general(left, right, (((1,), (0,)), ((), ())), preferred_element_type=F32)


def dot_nt(left, right):
    return lax.dot_general(left, right, (((1,), (1,)), ((), ())), preferred_element_type=F32)


def dot_tn(left, right):
    return lax.dot_general(left, right, (((0,), (0,)), ((), ())), preferred_element_type=F32)


def split_bf16(value, parts):
    pieces = []
    for _ in range(parts - 1):
        upper = value.astype(BF16)
        pieces.append(upper)
        value = value - upper.astype(F32)
    pieces.append(value.astype(BF16))
    return pieces


def head_rows(first_lane, width):
    lane = lax.broadcasted_iota(jnp.int32, (LANES, width), 1) + first_lane
    row = lax.broadcasted_iota(jnp.int32, (LANES, width), 0)
    return (lax.shift_right_logical(lane, 6) == row).astype(F32).astype(BF16)


def head_cols(first_lane, width):
    lane = lax.broadcasted_iota(jnp.int32, (width, LANES), 0) + first_lane
    col = lax.broadcasted_iota(jnp.int32, (width, LANES), 1)
    return (lax.shift_right_logical(lane, 6) == col).astype(F32).astype(BF16)


def spread(pieces, marks):
    total = dot_nn(pieces[0], marks)
    for piece in pieces[1:]:
        total = total + dot_nn(piece, marks)
    return total


def gather_heads(value, marks_t):
    upper, lower = split_bf16(value, 2)
    return dot_nn(upper, marks_t) + dot_nn(lower, marks_t)


def tri_rows(size, reverse=False):
    row = lax.broadcasted_iota(jnp.int32, (size, size), 0)
    col = lax.broadcasted_iota(jnp.int32, (size, size), 1)
    return (row <= col) if reverse else (row >= col)


def lane_tile(width):
    return 256 if width % 256 == 0 else LANES


def load_states(dst, src):
    count, _, rows, _ = src.shape
    for at in range(count):
        dst[at * rows : (at + 1) * rows, :] = src[at, 0].astype(F32)


def assemble(blocks, places):
    count = len(blocks)
    rows, cols = blocks[0].shape

    def body(place_ref, *refs):
        out, sems = refs[count], refs[count + 1]
        copies = [
            pltpu.make_async_copy(refs[at], out.at[place_ref[at]], sems.at[at]) for at in range(count)
        ]
        for copy in copies:
            copy.start()
        for copy in copies:
            copy.wait()

    return pl.pallas_call(
        body,
        grid_spec=pltpu.PrefetchScalarGridSpec(
            num_scalar_prefetch=1,
            grid=(1,),
            in_specs=[pl.BlockSpec(memory_space=pl.ANY)] * count,
            out_specs=pl.BlockSpec((count, rows, cols), lambda i, *_: (0, 0, 0)),
            scratch_shapes=[pltpu.SemaphoreType.DMA((count,))],
        ),
        out_shape=jax.ShapeDtypeStruct((count, rows, cols), BF16),
        name="assemble",
    )(places, *blocks).reshape(count * rows, cols)


def take_apart(grad, places, n):
    planes = n // 4
    n_even, n_odd = (planes + 1) // 2, planes // 2
    rows, cols = grad.shape[0] // n, grad.shape[1]
    shapes = [
        (n_even, 2, rows, cols),
        (n_even, rows, cols),
        (n_even, rows, cols),
        (n_odd, 2, rows, cols),
        (n_odd, rows, cols),
        (n_odd, rows, cols),
    ]

    def body(place_ref, src, *refs):
        outs, sems = refs[:6], refs[6]
        copies = []
        for plane in range(planes):
            at = plane // 2
            for near in range(4):
                step_y, step_x = near // 2, near % 2
                if plane % 2 == 0:
                    dst = outs[0].at[at, step_y] if step_x else outs[1 + step_y].at[at]
                else:
                    dst = outs[3].at[at, step_x] if step_y else outs[4 + step_x].at[at]
                index = plane * 4 + near
                copies.append(
                    pltpu.make_async_copy(src.at[place_ref[index]], dst, sems.at[index])
                )
        for copy in copies:
            copy.start()
        for copy in copies:
            copy.wait()

    return pl.pallas_call(
        body,
        grid_spec=pltpu.PrefetchScalarGridSpec(
            num_scalar_prefetch=1,
            grid=(1,),
            in_specs=[pl.BlockSpec((n, rows, cols), lambda i, *_: (0, 0, 0))],
            out_specs=[pl.BlockSpec(memory_space=pl.ANY)] * 6,
            scratch_shapes=[pltpu.SemaphoreType.DMA((n,))],
        ),
        out_shape=[jax.ShapeDtypeStruct(shape, BF16) for shape in shapes],
        name="take_apart",
    )(places, grad.reshape(n, rows, cols))


def row_block(rows, cols):
    return pl.BlockSpec((rows, cols), lambda m, *_: (m, 0))


def lead_block(rows, cols):
    return pl.BlockSpec((1, rows, cols), lambda m, *_: (m, 0, 0))


def whole_block(rows, cols):
    return pl.BlockSpec((rows, cols), lambda m, *_: (0, 0))


def state_block(n, nb, cols):
    return pl.BlockSpec((n, 1, nb, cols), lambda m, *_: (0, m, 0, 0))


def shape_of(shape, dtype):
    return jax.ShapeDtypeStruct(shape, dtype)


def conv_forward(scratch, base, taps, bias):
    pre = bias
    for tap_at in range(4):
        pre = pre + taps[tap_at : tap_at + 1] * scratch[base + 5 + tap_at : base + 5 + tap_at + BLOCK, :]
    return pre


def prep_kernel(keep_ref, bc_ref, dtin_ref, taps_ref, bias_ref, dtb_ref, neg_ref,
                bcin_ref, bcact_ref, dt_ref, cs_ref, sig_ref, cst_ref, ext):
    keep = keep_ref[pl.program_id(0)]
    low = bc_ref[...].astype(BF16).astype(F32)
    ext[0:HALO, :] = low[0:HALO, :] * keep
    ext[HALO:, :] = low[HALO:, :]
    bcin_ref[...] = ext[...].astype(BF16)
    pre = conv_forward(ext, 0, taps_ref[...], bias_ref[...])
    bcact_ref[...] = (pre * jax.nn.sigmoid(pre)).astype(BF16)
    raw = dtin_ref[HALO:, :] + dtb_ref[...]
    dt = jnp.maximum(raw, 0.0) + jnp.log1p(jnp.exp(-jnp.abs(raw)))
    dt_ref[...] = dt
    sig_ref[...] = jax.nn.sigmoid(raw)
    rate = dt * neg_ref[...]
    lower = tri_rows(BLOCK).astype(F32).astype(BF16)
    cs = jnp.zeros_like(rate)
    for piece in reversed(split_bf16(rate, 3)):
        cs = cs + dot_nn(lower, piece)
    cs_ref[...] = cs
    cst_ref[0] = cs.T


def project_kernel(keep_ref, normed_ref, w_ref, taps_ref, bias_ref, xin_ref, xmix_ref, ext):
    micro = keep_ref.shape[0]
    span = BLOCK + HALO
    ext[...] = dot_nn(normed_ref[...], w_ref[...]).astype(BF16).astype(F32)
    for m in range(micro):
        ext[m * span : m * span + HALO, :] = ext[m * span : m * span + HALO, :] * keep_ref[m]
    xin_ref[...] = ext[...].astype(BF16)
    for m in range(micro):
        pre = conv_forward(ext, m * span, taps_ref[...], bias_ref[...])
        xmix_ref[m * BLOCK : (m + 1) * BLOCK, :] = (pre * jax.nn.sigmoid(pre)).astype(BF16)


def end_state_kernel(x_ref, b_ref, dt_ref, cs_ref, out_ref):
    width = x_ref.shape[1]
    count, _, nb, _ = out_ref.shape
    tile = lane_tile(width)
    b_t = b_ref[...].astype(F32).T.astype(BF16)
    dt_p = split_bf16(dt_ref[...], 2)
    cs_p = split_bf16(cs_ref[...], 3)
    for c0 in range(0, width, tile):
        marks = head_rows(c0, tile)
        cs_x = spread(cs_p, marks)
        weight = jnp.exp(cs_x[BLOCK - 1 : BLOCK, :] - cs_x) * spread(dt_p, marks)
        xw = (x_ref[:, c0 : c0 + tile].astype(F32) * weight).astype(BF16)
        state = dot_nn(b_t, xw)
        for at in range(count):
            out_ref[at, 0, :, c0 : c0 + tile] = state[at * nb : (at + 1) * nb, :].astype(BF16)


def scan_kernel(reverse, deal_ref, first_ref, s_ref, lam_ref, out_ref, decay):
    count, micro, nb, width = s_ref.shape
    tile = lane_tile(width)
    for m in range(micro):
        pieces = split_bf16(lam_ref[m], 3)
        for c0 in range(0, width, tile):
            decay[m * count : (m + 1) * count, c0 : c0 + tile] = jnp.exp(
                spread(pieces, head_rows(c0, tile))
            )
    for m in range(micro):

        def step(at, state, m=m):
            p = count - 1 - at if reverse else at
            q = deal_ref[m * count + p]
            gain = 1.0 - first_ref[m * count + p].astype(F32)
            factor = decay[pl.ds(m * count + q, 1), :]
            own = s_ref[q, m].astype(F32)
            if reverse:
                out_ref[q, m] = state.astype(BF16)
                return (factor * state + own) * gain
            state = state * gain
            out_ref[q, m] = state.astype(BF16)
            return factor * state + own

        lax.fori_loop(0, count, step, jnp.zeros((nb, width), F32))


def intra_kernel(x_ref, b_ref, c_ref, dt_ref, cs_ref, cst_ref, y_ref, cb):
    width = x_ref.shape[1]
    cb[...] = jnp.where(tri_rows(BLOCK), dot_nt(c_ref[...], b_ref[...]), 0.0)
    dt_p = split_bf16(dt_ref[...], 2)
    cs_p = split_bf16(cs_ref[...], 3)
    left = lax.broadcasted_iota(jnp.int32, (BLOCK, LANES), 1) < HDIM

    def pair(g, carry):
        lanes = pl.ds(pl.multiple_of(g * LANES, LANES), LANES)
        marks = head_rows(g * LANES, LANES)
        cs_x = spread(cs_p, marks)
        xd = (x_ref[:, lanes].astype(F32) * spread(dt_p, marks)).astype(BF16)
        ys = []
        for e in range(2):
            gap = cs_x[:, e * HDIM : e * HDIM + 1] - cst_ref[0, pl.ds(2 * g + e, 1), :]
            mix = (cb[...] * jnp.exp(jnp.minimum(gap, 0.0))).astype(BF16)
            ys.append(dot_nn(mix, xd))
        y_ref[:, lanes] = jnp.where(left, ys[0], ys[1])
        return carry

    lax.fori_loop(0, width // LANES, pair, 0)


def stats_kernel(yin_ref, x_ref, c_ref, cs_ref, s_ref, gate_ref, db_ref, gain_ref, skip_ref,
                 y_ref, stat_ref, states):
    width = x_ref.shape[1]
    tile = lane_tile(width)
    load_states(states, s_ref)
    cs_p = split_bf16(cs_ref[...], 3)
    c_mat = c_ref[...]
    squares = jnp.zeros((BLOCK, tile), F32)
    crosses = jnp.zeros((BLOCK, tile), F32)
    for c0 in range(0, width, tile):
        sl = slice(c0, c0 + tile)
        outer = dot_nn(c_mat, states[:, sl].astype(BF16))
        decay = jnp.exp(spread(cs_p, head_rows(c0, tile)))
        y = yin_ref[:, sl] + decay * outer + skip_ref[:, sl] * x_ref[:, sl].astype(F32)
        y_ref[:, sl] = y
        gate = gate_ref[:, sl].astype(F32)
        gated = y * (gate * jax.nn.sigmoid(gate))
        squares = squares + gated * gated
        crosses = crosses + gated * (db_ref[:, sl] * gain_ref[:, sl])
    stat_ref[:, 0:1] = jnp.sum(squares, axis=1, keepdims=True)
    stat_ref[:, 1:2] = jnp.sum(crosses, axis=1, keepdims=True)


def gate_kernel(y_ref, c_ref, cs_ref, gate_ref, db_ref, gain_ref, stat_ref,
                branch_ref, dy_ref, dgate_ref, gg_ref, out_ref):
    width = y_ref.shape[1]
    count, _, nb, _ = out_ref.shape
    tile = lane_tile(width)
    cs_p = split_bf16(cs_ref[...], 3)
    c_t = c_ref[...].astype(F32).T.astype(BF16)
    root = lax.rsqrt(stat_ref[:, 0:1] / INNER + EPSILON)
    shift = root * stat_ref[:, 1:2] / INNER
    for c0 in range(0, width, tile):
        sl = slice(c0, c0 + tile)
        y = y_ref[:, sl]
        gate = gate_ref[:, sl].astype(F32)
        sig = jax.nn.sigmoid(gate)
        act = gate * sig
        scaled = y * act * root
        d_branch = db_ref[:, sl]
        gain = gain_ref[:, sl]
        branch_ref[:, sl] = (scaled * gain).astype(BF16)
        gg_ref[0, :, sl] = jnp.sum(d_branch * scaled, axis=0, keepdims=True)
        d_gated = root * (d_branch * gain - scaled * shift)
        dy = (d_gated * act).astype(BF16)
        dy_ref[:, sl] = dy
        dgate_ref[:, sl] = (d_gated * y * (sig * (1.0 + gate * (1.0 - sig)))).astype(BF16)
        decay = jnp.exp(spread(cs_p, head_rows(c0, tile)))
        state = dot_nn(c_t, (dy.astype(F32) * decay).astype(BF16))
        for at in range(count):
            out_ref[at, 0, :, sl] = state[at * nb : (at + 1) * nb, :].astype(BF16)


def intra_back_kernel(x_ref, dy_ref, b_ref, c_ref, dt_ref, cs_ref, cst_ref, y_ref, s_ref, skip_ref,
                      dxp_ref, db_ref, dc_ref, dcs_ref, ddt_ref, gs_ref,
                      cbt, acc, states):
    width = x_ref.shape[1]
    upper = tri_rows(BLOCK, reverse=True)
    cbt[...] = jnp.where(upper, dot_nt(b_ref[...], c_ref[...]), 0.0)
    acc[...] = jnp.zeros_like(acc)
    load_states(states, s_ref)
    dt_p = split_bf16(dt_ref[...], 2)
    cs_p = split_bf16(cs_ref[...], 3)
    left = lax.broadcasted_iota(jnp.int32, (BLOCK, LANES), 1) < HDIM
    dc_ref[...] = jnp.zeros_like(dc_ref)
    dcs_ref[...] = jnp.zeros_like(dcs_ref)
    ddt_ref[...] = jnp.zeros_like(ddt_ref)

    def pair(g, carry):
        lanes = pl.ds(pl.multiple_of(g * LANES, LANES), LANES)
        marks = head_rows(g * LANES, LANES)
        marks_t = head_cols(g * LANES, LANES)
        cs_x = spread(cs_p, marks)
        dt_x = spread(dt_p, marks)
        xf = x_ref[:, lanes].astype(F32)
        xd = (xf * dt_x).astype(BF16)
        xdf = xd.astype(F32)
        dy = dy_ref[:, lanes]
        dyf = dy.astype(F32)
        us = []
        total = acc[...]
        for e in range(2):
            gap = cst_ref[0, pl.ds(2 * g + e, 1), :] - cs_x[:, e * HDIM : e * HDIM + 1]
            decay = jnp.exp(jnp.minimum(gap, 0.0))
            half = jnp.where(left if e == 0 else ~left, xdf, 0.0).astype(BF16)
            total = total + dot_nt(half, dy) * decay
            us.append(dot_nn((cbt[...] * decay).astype(BF16), dy))
        acc[...] = total
        u = jnp.where(left, us[0], us[1])
        skip = skip_ref[:, lanes]
        dc_ref[...] += dot_nt((dyf * jnp.exp(cs_x)).astype(BF16), states[:, lanes].astype(BF16))
        dxp_ref[:, lanes] = dt_x * u + skip * dyf
        dcs_ref[...] += gather_heads(dyf * (y_ref[:, lanes] - skip * xf) - xdf * u, marks_t)
        ddt_ref[...] += gather_heads(xf * u, marks_t)
        gs_ref[0, :, lanes] = jnp.sum(dyf * xf, axis=0, keepdims=True)
        return carry

    lax.fori_loop(0, width // LANES, pair, 0)
    dcb_t = jnp.where(upper, acc[...], 0.0)
    db_ref[...] = dot_nn(dcb_t.astype(BF16), c_ref[...])
    dc_ref[...] += dot_nn(dcb_t.T.astype(BF16), b_ref[...])


def conv_back(ext, pad, d_act, taps, bias, keep):
    pre = conv_forward(ext, 0, taps, bias)
    sig = jax.nn.sigmoid(pre)
    d_pre = d_act * (sig * (1.0 + pre * (1.0 - sig)))
    pad[HALO : HALO + BLOCK, :] = d_pre
    g_taps = [
        jnp.sum(d_pre * ext[5 + tap_at : 5 + tap_at + BLOCK, :], axis=0, keepdims=True)
        for tap_at in range(4)
    ]
    g_bias = jnp.sum(d_pre, axis=0, keepdims=True)
    span = BLOCK + HALO
    d_in = taps[0:1] * pad[3 : 3 + span, :]
    for tap_at in range(1, 4):
        d_in = d_in + taps[tap_at : tap_at + 1] * pad[3 - tap_at : 3 - tap_at + span, :]
    row = lax.broadcasted_iota(jnp.int32, d_in.shape, 0)
    return d_in * jnp.where(row < HALO, keep, 1.0), g_taps, g_bias


def state_back_kernel(keep_ref, x_ref, b_ref, dt_ref, cs_ref, sig_ref, neg_ref, s_ref, ds_ref, dxp_ref,
                      dbp_ref, dcp_ref, dcs_ref, ddt_ref, xin_ref, taps_ref, bias_ref,
                      dx_ref, dbc_ref, ddtin_ref, gt_ref, gb_ref, ga_ref, gd_ref,
                      states, d_states, ext, pad):
    width = x_ref.shape[1]
    tile = lane_tile(width)
    keep = keep_ref[pl.program_id(0)]
    load_states(states, s_ref)
    load_states(d_states, ds_ref)
    dt = dt_ref[...]
    cs = cs_ref[...]
    dt_p = split_bf16(dt, 2)
    cs_p = split_bf16(cs, 3)
    b_mat = b_ref[...]
    d_b = dbp_ref[...]
    d_wend = jnp.zeros((BLOCK, LANES), F32)
    d_lam = jnp.zeros((8, LANES), F32)
    pad[0:HALO, :] = jnp.zeros((HALO, tile), F32)
    pad[HALO + BLOCK :, :] = jnp.zeros((HALO, tile), F32)
    for c0 in range(0, width, tile):
        sl = slice(c0, c0 + tile)
        marks = head_rows(c0, tile)
        marks_t = head_cols(c0, tile)
        ds_low = d_states[:, sl].astype(BF16)
        along = dot_nn(b_mat, ds_low)
        cs_x = spread(cs_p, marks)
        lam_x = cs_x[BLOCK - 1 : BLOCK, :]
        weight = jnp.exp(lam_x - cs_x) * spread(dt_p, marks)
        xf = x_ref[:, sl].astype(F32)
        d_b = d_b + dot_nt((xf * weight).astype(BF16), ds_low)
        d_wend = d_wend + gather_heads(along * xf, marks_t)
        cross = jnp.sum(d_states[:, sl] * states[:, sl], axis=0, keepdims=True) * jnp.exp(lam_x)
        d_lam = d_lam + gather_heads(jnp.broadcast_to(cross, (8, tile)), marks_t)
        ext[...] = xin_ref[:, sl].astype(F32)
        d_in, g_taps, g_bias = conv_back(
            ext, pad, dxp_ref[:, sl] + weight * along, taps_ref[:, sl], bias_ref[:, sl], keep
        )
        dx_ref[:, sl] = d_in.astype(BF16)
        for tap_at in range(4):
            gt_ref[0, tap_at : tap_at + 1, sl] = g_taps[tap_at]
        gb_ref[0, :, sl] = g_bias
    dbc_ref[:, :STATE] = d_b.astype(BF16)
    dbc_ref[:, STATE:] = dcp_ref[...].astype(BF16)
    fade = jnp.exp(cs[BLOCK - 1 : BLOCK, :] - cs)
    end_gain = d_wend * (fade * dt)
    d_cs = dcs_ref[...] - end_gain
    last = jnp.sum(end_gain, axis=0, keepdims=True) + d_lam[0:1, :]
    row = lax.broadcasted_iota(jnp.int32, d_cs.shape, 0)
    d_cs = d_cs + jnp.where(row == BLOCK - 1, last, 0.0)
    upper = tri_rows(BLOCK, reverse=True).astype(F32).astype(BF16)
    d_rate = jnp.zeros_like(d_cs)
    for piece in reversed(split_bf16(d_cs, 3)):
        d_rate = d_rate + dot_nn(upper, piece)
    neg = neg_ref[...]
    d_in = (ddt_ref[...] + d_wend * fade + d_rate * neg) * sig_ref[...]
    ddtin_ref[0:HALO, :] = jnp.zeros((HALO, LANES), BF16)
    ddtin_ref[HALO:, :] = d_in.astype(BF16)
    gd_ref[0] = jnp.sum(d_in, axis=0, keepdims=True)
    ga_ref[0] = jnp.sum(d_rate * dt, axis=0, keepdims=True) * neg


def bc_back_kernel(keep_ref, dbc_ref, bcin_ref, taps_ref, bias_ref, out_ref, gt_ref, gb_ref, ext, pad):
    keep = keep_ref[pl.program_id(0)]
    width = bcin_ref.shape[1]
    pad[0:HALO, :] = jnp.zeros((HALO, width), F32)
    pad[HALO + BLOCK :, :] = jnp.zeros((HALO, width), F32)
    ext[...] = bcin_ref[...].astype(F32)
    d_in, g_taps, g_bias = conv_back(
        ext, pad, dbc_ref[...].astype(F32), taps_ref[...], bias_ref[...], keep
    )
    out_ref[...] = d_in.astype(BF16)
    for tap_at in range(4):
        gt_ref[0, tap_at : tap_at + 1, :] = g_taps[tap_at]
    gb_ref[0] = g_bias


def run_kernel(body, name, grid, scalars, operands, in_specs, out_specs, out_shape, scratch=()):
    return pl.pallas_call(
        body,
        grid_spec=pltpu.PrefetchScalarGridSpec(
            num_scalar_prefetch=len(scalars),
            grid=grid,
            in_specs=in_specs,
            out_specs=out_specs,
            scratch_shapes=list(scratch),
        ),
        out_shape=out_shape,
        name=name,
    )(*scalars, *operands)


def pad_lanes(value, width):
    extra = width - value.shape[-1]
    if extra == 0:
        return value
    return jnp.pad(value, [(0, 0)] * (value.ndim - 1) + [(0, extra)])


def per_device(
    hidden,
    cotangent,
    z_proj,
    x_proj,
    bc_proj,
    dt_proj,
    out_proj,
    conv_x,
    conv_x_bias,
    conv_bc,
    conv_bc_bias,
    dt_bias,
    a_log,
    d_skip,
    norm_gain,
    gate_gain,
    lengths,
    dealing,
):
    n = lax.axis_size("seq")
    n_head = lax.axis_size("head")
    seq_at = lax.axis_index("seq")
    head_at = lax.axis_index("head")
    micro = lengths.shape[0]
    width = z_proj.shape[1]
    bc_loc = bc_proj.shape[1]
    heads = dt_proj.shape[1]
    portion = MODEL_WIDTH // n_head
    own = MODEL_WIDTH // n
    planes = n // 4
    nb = STATE // n
    rows = micro * BLOCK
    span = BLOCK + HALO
    rows_ext = micro * span
    bc_pad = -(-bc_loc // LANES) * LANES
    in_width = width + bc_pad + LANES

    def swap(value, bit):
        return lax.ppermute(value, "seq", [(i, i ^ bit) for i in range(n)])

    def plane_shift(value, k):
        return lax.ppermute(value, "seq", [(i, (i + 4 * k) % n) for i in range(n)])

    def all_to_all(value):
        return lax.all_to_all(value, "seq", 0, 0, tiled=False)

    order = jnp.arange(n, dtype=jnp.int32)
    run_ends = jnp.cumsum(lengths, axis=1)
    first = jnp.any((run_ends - lengths)[:, :, None] == order[None, None, :], axis=1)
    pos = jnp.sum(jnp.where(dealing == seq_at, order[None], 0), axis=1)
    at_pos = order[None] == pos[:, None]
    keep = 1.0 - jnp.sum(jnp.where(at_pos, first, False).astype(F32), axis=1)
    pred_dev = jnp.sum(jnp.where(order[None] == jnp.maximum(pos - 1, 0)[:, None], dealing, 0), axis=1)
    succ_dev = jnp.sum(jnp.where(order[None] == jnp.minimum(pos + 1, n - 1)[:, None], dealing, 0), axis=1)
    has_next = (pos + 1 < n).astype(F32)
    first_flat = first.astype(jnp.int32).reshape(-1)
    deal_flat = dealing.reshape(-1)
    z_at, near_at = seq_at // 4, seq_at % 4
    from_places = jnp.stack(
        [((z_at - k) % planes) * 4 + (near_at ^ near) for k in range(planes) for near in range(4)]
    ).astype(jnp.int32)
    to_places = jnp.stack(
        [((z_at + k) % planes) * 4 + (near_at ^ near) for k in range(planes) for near in range(4)]
    ).astype(jnp.int32)

    def gather_rows(block):
        layers = [block] + [plane_shift(block, k) for k in range(1, planes)]
        blocks = []
        for k, layer in enumerate(layers):
            by_x, by_y = swap(layer, 1), swap(layer, 2)
            far = swap(by_y, 1) if k % 2 == 0 else swap(by_x, 2)
            blocks += [layer, by_x, by_y, far]
        return assemble(blocks, from_places)

    def scatter_rows(grad):
        x_send, x_keep0, x_keep1, y_send, y_keep0, y_keep1 = take_apart(grad, to_places, n)
        x_got, y_got = swap(x_send, 1), swap(y_send, 2)
        y_next = (x_keep1.astype(F32) + x_got[:, 1].astype(F32)).astype(BF16)
        x_next = (y_keep1.astype(F32) + y_got[:, 1].astype(F32)).astype(BF16)
        y_last, x_last = swap(y_next, 2), swap(x_next, 1)
        even = x_keep0.astype(F32) + x_got[:, 0].astype(F32) + y_last.astype(F32)
        odd = y_keep0.astype(F32) + y_got[:, 0].astype(F32) + x_last.astype(F32)
        total = even[0]
        for k in range(1, planes):
            part = (odd if k % 2 else even)[k // 2]
            total = total + plane_shift(part.astype(BF16), k).astype(F32)
        return total

    group = jnp.concatenate([x_proj, pad_lanes(bc_proj, bc_pad), pad_lanes(dt_proj, LANES)], axis=1)
    w_in = gather_rows(group)
    w_z = gather_rows(z_proj)
    w_out = lax.all_gather(out_proj, "seq", axis=0, tiled=True)
    hidden3 = hidden.reshape(micro, BLOCK, MODEL_WIDTH)
    tails = hidden3[:, BLOCK - 3 :].reshape(micro * 3, MODEL_WIDTH)
    tails_all = all_to_all(jnp.broadcast_to(tails[None], (n, micro * 3, MODEL_WIDTH)))
    halo = jnp.stack(
        [
            lax.dynamic_slice(tails_all, (pred_dev[m], 3 * m, 0), (1, 3, MODEL_WIDTH))[0]
            for m in range(micro)
        ]
    )

    def normalize(value):
        value = value.astype(F32)
        root = lax.rsqrt(jnp.mean(value * value, axis=-1, keepdims=True) + EPSILON)
        return value * root, root

    x_hat, inv_rms = normalize(hidden)
    normed = (x_hat * norm_gain).astype(BF16)
    normed_halo = (normalize(halo)[0] * norm_gain).astype(BF16)
    normed_ext = jnp.concatenate(
        [
            jnp.zeros((micro, HALO - 3, MODEL_WIDTH), BF16),
            normed_halo,
            normed.reshape(micro, BLOCK, MODEL_WIDTH),
        ],
        axis=1,
    ).reshape(rows_ext, MODEL_WIDTH)

    neg_rate = pad_lanes(-jnp.exp(a_log)[None], LANES)
    dtb = pad_lanes(dt_bias[None], LANES)
    skip = jnp.repeat(d_skip, HDIM)[None]
    taps_bc, bias_bc = pad_lanes(conv_bc, bc_pad), pad_lanes(conv_bc_bias[None], bc_pad)
    bc_raw = dot_nn(normed_ext, w_in[:, width : width + bc_pad])
    dt_raw = dot_nn(normed_ext, w_in[:, width + bc_pad :])
    bc_in, bc_act, dt, cs, sig, cs_t = run_kernel(
        prep_kernel, "prep", (micro,), (keep,),
        (bc_raw, dt_raw, taps_bc, bias_bc, dtb, neg_rate),
        [row_block(span, bc_pad), row_block(span, LANES), whole_block(4, bc_pad), whole_block(1, bc_pad),
         whole_block(1, LANES), whole_block(1, LANES)],
        [row_block(span, bc_pad), row_block(BLOCK, bc_pad)] + [row_block(BLOCK, LANES)] * 3
        + [lead_block(LANES, BLOCK)],
        [shape_of((rows_ext, bc_pad), BF16), shape_of((rows, bc_pad), BF16)]
        + [shape_of((rows, LANES), F32)] * 3 + [shape_of((micro, LANES, BLOCK), F32)],
        [pltpu.VMEM((span, bc_pad), F32)],
    )
    bc_all = lax.all_gather(bc_act[:, :bc_loc], "head", axis=1, tiled=True)
    b_mat, c_mat = bc_all[:, :STATE], bc_all[:, STATE:]
    lam = cs.reshape(micro, BLOCK, LANES)[:, BLOCK - 1]
    lam_all = all_to_all(jnp.broadcast_to(lam[None], (n, micro, LANES))).transpose(1, 0, 2)
    tile = lane_tile(width)
    x_in, x_mix = run_kernel(
        project_kernel, "project", (width // tile,), (keep,),
        (normed_ext, w_in, conv_x, conv_x_bias[None]),
        [pl.BlockSpec((rows_ext, MODEL_WIDTH), lambda c, *_: (0, 0)),
         pl.BlockSpec((MODEL_WIDTH, tile), lambda c, *_: (0, c)),
         pl.BlockSpec((4, tile), lambda c, *_: (0, c)),
         pl.BlockSpec((1, tile), lambda c, *_: (0, c))],
        [pl.BlockSpec((rows_ext, tile), lambda c, *_: (0, c)),
         pl.BlockSpec((rows, tile), lambda c, *_: (0, c))],
        [shape_of((rows_ext, width), BF16), shape_of((rows, width), BF16)],
        [pltpu.VMEM((rows_ext, tile), F32)],
    )

    x_block = row_block(BLOCK, width)
    head_block = row_block(BLOCK, LANES)
    states_block = state_block(n, nb, width)
    states_shape = shape_of((n, micro, nb, width), BF16)

    def exchange(payload, reverse):
        got = all_to_all(payload)
        scanned = pl.pallas_call(
            lambda *refs: scan_kernel(reverse, *refs),
            grid_spec=pltpu.PrefetchScalarGridSpec(
                num_scalar_prefetch=2,
                grid=(1,),
                in_specs=[pl.BlockSpec((n, micro, nb, width), lambda m, *_: (0, 0, 0, 0)),
                          pl.BlockSpec((micro, n, LANES), lambda m, *_: (0, 0, 0))],
                out_specs=pl.BlockSpec((n, micro, nb, width), lambda m, *_: (0, 0, 0, 0)),
                scratch_shapes=[pltpu.VMEM((micro * n, width), F32)],
            ),
            out_shape=states_shape,
            name="scan_back" if reverse else "scan",
        )(deal_flat, first_flat, got, lam_all)
        return all_to_all(scanned)

    end_states = run_kernel(
        end_state_kernel, "end_state", (micro,), (),
        (x_mix, b_mat, dt, cs),
        [x_block, head_block, head_block, head_block],
        states_block, states_shape,
    )
    s_in = exchange(end_states, False)
    y_intra = run_kernel(
        intra_kernel, "intra", (micro,), (),
        (x_mix, b_mat, c_mat, dt, cs, cs_t),
        [x_block, head_block, head_block, head_block, head_block, lead_block(LANES, BLOCK)],
        x_block, shape_of((rows, width), F32),
        [pltpu.VMEM((BLOCK, BLOCK), F32)],
    )
    gate = dot_nn(normed, w_z).astype(BF16)
    d_branch = dot_nn(cotangent, w_out)
    gain = gate_gain[None]
    gain_block = whole_block(1, width)
    y, stats = run_kernel(
        stats_kernel, "stats", (micro,), (),
        (y_intra, x_mix, c_mat, cs, s_in, gate, d_branch, gain, skip),
        [x_block, x_block, head_block, head_block, states_block, x_block, x_block, gain_block, gain_block],
        [x_block, row_block(BLOCK, 2)],
        [shape_of((rows, width), F32), shape_of((rows, 2), F32)],
        [pltpu.VMEM((STATE, width), F32)],
    )
    totals = jnp.sum(lax.all_gather(stats, "head", axis=0), axis=0)
    branch, d_y, d_gate, g_gate, d_entry = run_kernel(
        gate_kernel, "gate", (micro,), (),
        (y, c_mat, cs, gate, d_branch, gain, totals),
        [x_block, head_block, head_block, x_block, x_block, gain_block, row_block(BLOCK, 2)],
        [x_block, x_block, x_block, lead_block(1, width), states_block],
        [shape_of((rows, width), BF16)] * 3 + [shape_of((micro, 1, width), F32), states_shape],
    )
    d_state = exchange(d_entry, True)

    partial_out = dot_nt(branch, w_out)
    out_piece = lax.psum_scatter(
        partial_out.astype(BF16), "head", scatter_dimension=1, tiled=True
    ).astype(F32)
    hidden_share = lax.dynamic_slice_in_dim(hidden, head_at * portion, portion, 1).astype(F32)
    block_out = (hidden_share + out_piece).astype(BF16)
    grad_out = scatter_rows(dot_tn(cotangent, branch).astype(BF16))
    grad_z = scatter_rows(dot_tn(normed, d_gate).astype(BF16))

    dx_part, db_part, dc_part, dcs_part, ddt_part, g_skip = run_kernel(
        intra_back_kernel, "intra_back", (micro,), (),
        (x_mix, d_y, b_mat, c_mat, dt, cs, cs_t, y, s_in, skip),
        [x_block, x_block, head_block, head_block, head_block, head_block, lead_block(LANES, BLOCK),
         x_block, states_block, gain_block],
        [x_block, head_block, head_block, head_block, head_block, lead_block(1, width)],
        [shape_of((rows, width), F32)] + [shape_of((rows, LANES), F32)] * 4
        + [shape_of((micro, 1, width), F32)],
        [pltpu.VMEM((BLOCK, BLOCK), F32), pltpu.VMEM((BLOCK, BLOCK), F32), pltpu.VMEM((STATE, width), F32)],
    )
    d_x, d_bc, d_dt, g_taps, g_bias, g_alog, g_dtb = run_kernel(
        state_back_kernel, "state_back", (micro,), (keep,),
        (x_mix, b_mat, dt, cs, sig, neg_rate, s_in, d_state, dx_part, db_part, dc_part, dcs_part, ddt_part,
         x_in, conv_x, conv_x_bias[None]),
        [x_block, head_block, head_block, head_block, head_block, whole_block(1, LANES), states_block,
         states_block, x_block, head_block, head_block, head_block, head_block, row_block(span, width),
         whole_block(4, width), whole_block(1, width)],
        [row_block(span, width), row_block(BLOCK, 2 * STATE), row_block(span, LANES), lead_block(4, width),
         lead_block(1, width), lead_block(1, LANES), lead_block(1, LANES)],
        [shape_of((rows_ext, width), BF16), shape_of((rows, 2 * STATE), BF16), shape_of((rows_ext, LANES), BF16),
         shape_of((micro, 4, width), F32), shape_of((micro, 1, width), F32), shape_of((micro, 1, LANES), F32),
         shape_of((micro, 1, LANES), F32)],
        [pltpu.VMEM((STATE, width), F32), pltpu.VMEM((STATE, width), F32), pltpu.VMEM((span, tile), F32),
         pltpu.VMEM((span + HALO, tile), F32)],
    )
    d_bc_own = lax.psum_scatter(d_bc, "head", scatter_dimension=1, tiled=True)
    d_bc_ext, g_taps_bc, g_bias_bc = run_kernel(
        bc_back_kernel, "bc_back", (micro,), (keep,),
        (pad_lanes(d_bc_own, bc_pad), bc_in, taps_bc, bias_bc),
        [row_block(BLOCK, bc_pad), row_block(span, bc_pad), whole_block(4, bc_pad), whole_block(1, bc_pad)],
        [row_block(span, bc_pad), lead_block(4, bc_pad), lead_block(1, bc_pad)],
        [shape_of((rows_ext, bc_pad), BF16), shape_of((micro, 4, bc_pad), F32), shape_of((micro, 1, bc_pad), F32)],
        [pltpu.VMEM((span, bc_pad), F32), pltpu.VMEM((span + HALO, bc_pad), F32)],
    )
    d_group = jnp.concatenate([d_x, d_bc_ext, d_dt], axis=1)
    grad_in = scatter_rows(dot_tn(normed_ext, d_group).astype(BF16))

    d_normed_ext = dot_nt(d_group, w_in).reshape(micro, span, MODEL_WIDTH)
    edges = d_normed_ext[:, HALO - 3 : HALO].reshape(micro * 3, MODEL_WIDTH).astype(BF16)
    edges_all = all_to_all(jnp.broadcast_to(edges[None], (n, micro * 3, MODEL_WIDTH)))
    incoming = jnp.stack(
        [
            lax.dynamic_slice(edges_all, (succ_dev[m], 3 * m, 0), (1, 3, MODEL_WIDTH))[0].astype(F32)
            * has_next[m]
            for m in range(micro)
        ]
    )
    d_normed = dot_nt(d_gate, w_z) + (
        d_normed_ext[:, HALO:] + jnp.pad(incoming, ((0, 0), (BLOCK - 3, 0), (0, 0)))
    ).reshape(rows, MODEL_WIDTH)
    piece = lax.psum_scatter(
        d_normed.astype(BF16), "head", scatter_dimension=1, tiled=True
    ).astype(F32)
    x_hat_share = hidden_share * inv_rms
    gain_share = lax.dynamic_slice_in_dim(norm_gain, head_at * portion, portion, 0)
    d_hat = piece * gain_share
    g_norm = jnp.sum(piece * x_hat_share, axis=0)
    row_stat = jnp.sum(
        lax.all_gather(jnp.sum(d_hat * x_hat_share, axis=1), "head", axis=0), axis=0
    )
    cot_share = lax.dynamic_slice_in_dim(cotangent, head_at * portion, portion, 1).astype(F32)
    grad_hidden = inv_rms * (d_hat - x_hat_share * (row_stat / MODEL_WIDTH)[:, None]) + cot_share

    small = [
        jnp.sum(g_taps, axis=0),
        jnp.sum(g_bias, axis=0),
        jnp.sum(g_taps_bc, axis=0)[:, :bc_loc],
        jnp.sum(g_bias_bc, axis=0)[:, :bc_loc],
        jnp.sum(g_dtb, axis=0)[:, :heads],
        jnp.sum(g_alog, axis=0)[:, :heads],
        jnp.sum(jnp.sum(g_skip, axis=0).reshape(heads, HDIM), axis=1),
        g_norm,
        jnp.sum(g_gate, axis=0),
    ]
    flat = jnp.concatenate([item.reshape(-1) for item in small])
    length = flat.shape[0]
    flat = jnp.pad(flat, (0, -length % 1024)).reshape(-1, LANES)
    bit = 1
    while bit < n:
        flat = flat + swap(flat, bit)
        bit *= 2
    flat = flat.reshape(-1)
    sums, at = [], 0
    for item in small:
        sums.append(flat[at : at + item.size].reshape(item.shape))
        at += item.size
    return (
        block_out,
        grad_hidden,
        grad_z,
        grad_in[:, :width],
        grad_in[:, width : width + bc_loc],
        grad_in[:, width + bc_pad : width + bc_pad + heads],
        grad_out,
        sums[0],
        sums[1].reshape(-1),
        sums[2],
        sums[3].reshape(-1),
        sums[4].reshape(-1),
        sums[5].reshape(-1),
        sums[6],
        sums[7],
        sums[8].reshape(-1),
    )


def solution(mesh):
    return jax.shard_map(
        per_device,
        mesh=mesh,
        in_specs=(
            P("seq", None),
            P("seq", None),
            P("seq", "head"),
            P("seq", "head"),
            P("seq", "head"),
            P("seq", "head"),
            P("seq", "head"),
            P(None, "head"),
            P("head"),
            P(None, "head"),
            P("head"),
            P("head"),
            P("head"),
            P("head"),
            P(),
            P("head"),
            P(),
            P(),
        ),
        out_specs=(
            P("seq", "head"),
            P("seq", "head"),
            P("seq", "head"),
            P("seq", "head"),
            P("seq", "head"),
            P("seq", "head"),
            P("seq", "head"),
            P(None, "head"),
            P("head"),
            P(None, "head"),
            P("head"),
            P("head"),
            P("head"),
            P("head"),
            P("head"),
            P("head"),
        ),
        check_vma=False,
    )
```

time: 1500 us -> 671 us (0.45)
  waiting for transfers between devices: 622 us -> 224 us
  blocking collectives: 375 us -> 35.5 us
  Pallas kernels: 0 us -> 127 us
  matrix products: 170 us -> 52.7 us
  starting transfers between devices: 0.83 us -> 109 us
  other arithmetic: 144 us -> 39.2 us
  local copies, waits for them, and re-layouts: 147 us -> 51.8 us
    all_gather x7 -> x1, waiting for transfers between devices: 307 us -> 0.01 us  [per_device(): w_out = lax.all_gather(out_proj, 'seq', axis=0, tiled=True)]
    unnamed x17 -> x5, waiting for transfers between devices: 314 us -> 8.26 us
    all_gather x8 -> x3, blocking collectives: 251 us -> 6.36 us  [the longest x1 2.39 us: per_device(): totals = jnp.sum(lax.all_gather(stats, 'head', axis=0), axis=0)]
    ppermute x0 -> x55, waiting for transfers between devices: none -> 184 us  [the longest x40 137 us: swap(): return lax.ppermute(value, 'seq', [(i, i ^ bit) for i in range(n)])]
    pallas_call x0 -> x16, Pallas kernels: none -> 127 us  [the longest x9 92.8 us: run_kernel(): pl.pallas_call(body, grid_spec=pltpu.PrefetchScalarGridSpec(num_scalar_pr...]
    dot_general x60 -> x10, matrix products: 170 us -> 52.7 us  [the longest x4 18.2 us: dot_nn(): lax.dot_general(left, right, (((1,), (0,)), ((), ())), preferred_element_...]
    psum x4 -> x0, blocking collectives: 84.9 us -> none  [the longest x1 75.5 us: per_device(): lax.psum((g_conv, g_conv_bias, g_dt_bias, g_a_log, g_skip, norm_gain_grad...]
    ppermute x0 -> x55, starting transfers between devices: none -> 69.3 us  [the longest x40 44.9 us: swap(): return lax.ppermute(value, 'seq', [(i, i ^ bit) for i in range(n)])]
  transfers between devices with their start and end apart: 15 -> 65, of which waited for: 7 -> 23; matrix products, arithmetic and copies ran while one was open for 26% -> 17% of each run, Pallas kernels for 0% -> 14%
where the time goes in v1:
time: 671 us; the launch traced here: 662 us
  waiting for transfers between devices  224 us (33%)
  Pallas kernels  127 us (19%)
  starting transfers between devices  109 us (16%)
  matrix products  52.7 us (8%)
  local copies, waits for them, and re-layouts  51.8 us (8%)
  other arithmetic  39.2 us (6%)
  blocking collectives  35.5 us (5%)
  between operations  23.1 us (3%)
    ppermute x40, waiting for transfers between devices, swap(): return lax.ppermute(value, 'seq', [(i, i ^ bit) for i in range(n)])  137 us
    pallas_call x9, Pallas kernels, run_kernel(): pl.pallas_call(body, grid_spec=pltpu.PrefetchScalarGridSpec(num_scalar_pr...  92.8 us
    ppermute x15, waiting for transfers between devices, plane_shift(): return lax.ppermute(value, 'seq', [(i, (i + 4 * k) % n) for i in range(n)])  46.1 us
    ppermute x40, starting transfers between devices, swap(): return lax.ppermute(value, 'seq', [(i, i ^ bit) for i in range(n)])  44.9 us
    all_to_all x6, starting transfers between devices, all_to_all(): return lax.all_to_all(value, 'seq', 0, 0, tiled=False)  38.5 us
    all_to_all x6, waiting for transfers between devices, all_to_all(): return lax.all_to_all(value, 'seq', 0, 0, tiled=False)  31.8 us
    all_to_all x1, blocking collectives, all_to_all(): return lax.all_to_all(value, 'seq', 0, 0, tiled=False)  29.2 us
    ppermute x15, starting transfers between devices, plane_shift(): return lax.ppermute(value, 'seq', [(i, (i + 4 * k) % n) for i in range(n)])  24.4 us
  transfers between devices with their start and end apart: 65, of which 23 were waited for; matrix products, arithmetic and copies ran while one was open for 17% of the time, Pallas kernels for 14%

profile of v1, /device:TPU:0, one launch (start us, length us, event | category | flops | bytes accessed | tf_op | source)
XLA Modules:
  0.0 661.8 jit_solution(4003548196471621964)
XLA Ops:
  9.8 4.1 collective-permute-start.7
  20.5 4.5 all-to-all-start
  37.4 23.3 %all-to-all-done = bf16[16,6,1536]{2,1,0:T(8,128)(2,1)S(1)} async-done(((bf16[16,6,1536]{2,1,0:T(8,128)(2,1)}), bf16[16,6,1536]{2,1,0:T(8,128)(2,1)S(1)}, u32[]{:S(2)}, u32[]{:S(2)}) %all-to-all-start) | async-done | bytes 294944 | tf_op jit(solution)/shard_map/all_to_all | solution.py:550
  60.8 2.4 collective-permute-start.13
  65.8 18.1 %collective-permute-done.9.refs_10_ = bf16[96,1792]{1,0:T(8,128)(2,1)S(1)} collective-permute-done((bf16[96,1792]{1,0:T(8,128)(2,1)}, bf16[96,1792]{1,0:T(8,128)(2,1)S(1)}, u32[]{:S(2)}, u32[]{:S(2)}) %collective-permute-start.9) | collective-permute-done | bytes 344096 | tf_op jit(solution)/shard_map/ppermute | solution.py:544
  91.3 10.9 %collective-permute-done.8.refs_9_ = bf16[96,1792]{1,0:T(8,128)(2,1)S(1)} collective-permute-done((bf16[96,1792]{1,0:T(8,128)(2,1)}, bf16[96,1792]{1,0:T(8,128)(2,1)S(1)}, u32[]{:S(2)}, u32[]{:S(2)}) %collective-permute-start.8) | collective-permute-done | bytes 344096 | tf_op jit(solution)/shard_map/ppermute | solution.py:544
  102.1 14.7 %collective-permute-done.2.refs_3_ = bf16[96,1792]{1,0:T(8,128)(2,1)S(1)} collective-permute-done((bf16[96,1792]{1,0:T(8,128)(2,1)}, bf16[96,1792]{1,0:T(8,128)(2,1)S(1)}, u32[]{:S(2)}, u32[]{:S(2)}) %collective-permute-start.2) | collective-permute-done | bytes 344096 | tf_op jit(solution)/shard_map/ppermute | solution.py:544
  116.9 6.4 collective-permute-done.10.refs_11_
  124.8 5.8 assemble.2
  130.6 2.3 fusion.38.dtin_ref
  132.9 2.3 fusion.40.bc_ref
  135.2 3.3 prep.1
  139.8 7.6 %all-to-all-start.2 = ((f32[16,2,128]{2,1,0:T(2,128)}), f32[16,2,128]{2,1,0:T(2,128)S(1)}, u32[]{:S(2)}, u32[]{:S(2)}) async-start(f32[16,2,128]{2,1,0:T(2,128)} %broadcast_in_dim.81), calls=%async_computation.2 | async-start | bytes 32768 | tf_op jit(solution)/shard_map/all_to_all | solution.py:550
  150.3 9.7 %project.1 = (bf16[528,1536]{1,0:T(8,128)(2,1)}, bf16[512,1536]{1,0:T(8,128)(2,1)}) custom-call(f32[2]{0:T(128)} %broadcast_subtract_fusion.keep_ref, bf16[528,1536]{1,0:T(8,128)(2,1)} %bitcast.201, bf16[1536,1792]{1,0:T(8,128)(2,1)} %bitcast.205, f32[4,1536]{1,0:T(4,128)} %taps_ref.6, f32[1,1536]{1,0:T(1,128)} %broadcast_in_dim.44.bias_ref), custom_call_target="tpu_custom_call" | custom-call | tf_op jit(solution)/shard_map/project/pallas_call | solution.py:484
  160.0 7.5 %end_state.1 = bf16[16,2,8,1536]{3,2,1,0:T(8,128)(2,1)} custom-call(bf16[512,1536]{1,0:T(8,128)(2,1)} %get-tuple-element.65.x_ref, bf16[512,128]{1,0:T(8,128)(2,1)} %get-tuple-element.195.b_ref, f32[512,128]{1,0:T(8,128)} %get-tuple-element.67.dt_ref, f32[512,128]{1,0:T(8,128)} %get-tuple-element.68.cs_ref), custom_call_target="tpu_custom_call" | custom-call | tf_op jit(solution)/shard_map/end_state/pallas_call | solution.py:484
  167.5 6.9 %all-to-all-start.1 = ((bf16[16,2,8,1536]{3,2,1,0:T(8,128)(2,1)}), bf16[16,2,8,1536]{3,2,1,0:T(8,128)(2,1)S(1)}, u32[]{:S(2)}, u32[]{:S(2)}) async-start(bf16[16,2,8,1536]{3,2,1,0:T(8,128)(2,1)} %end_state.1), calls=%async_computation.1 | async-start | bytes 1572864 | tf_op jit(solution)/shard_map/all_to_all | solution.py:550
  176.4 2.4 collective-permute-start.22
  183.2 15.7 %collective-permute-done.18.refs_4_ = bf16[96,1536]{1,0:T(8,128)(2,1)S(1)} collective-permute-done((bf16[96,1536]{1,0:T(8,128)(2,1)S(1)}, bf16[96,1536]{1,0:T(8,128)(2,1)S(1)}, u32[]{:S(2)}, u32[]{:S(2)}) %collective-permute-start.18) | collective-permute-done | bytes 294944 | tf_op jit(solution)/shard_map/ppermute | solution.py:547
  200.3 14.4 %collective-permute-done.22.refs_8_ = bf16[96,1536]{1,0:T(8,128)(2,1)S(1)} collective-permute-done((bf16[96,1536]{1,0:T(8,128)(2,1)S(1)}, bf16[96,1536]{1,0:T(8,128)(2,1)S(1)}, u32[]{:S(2)}, u32[]{:S(2)}) %collective-permute-start.22) | collective-permute-done | bytes 294944 | tf_op jit(solution)/shard_map/ppermute | solution.py:547
  220.3 4.5 collective-permute-done.24.refs_10_
  227.7 3.3 collective-permute-done.20.refs_6_
  239.3 3.6 scan.1
  242.9 9.2 %all-to-all-start.3 = ((bf16[16,2,8,1536]{3,2,1,0:T(8,128)(2,1)}), bf16[16,2,8,1536]{3,2,1,0:T(8,128)(2,1)S(1)}, u32[]{:S(2)}, u32[]{:S(2)}) async-start(bf16[16,2,8,1536]{3,2,1,0:T(8,128)(2,1)} %scan.1), calls=%async_computation.3 | async-start | bytes 1572864 | tf_op jit(solution)/shard_map/all_to_all | solution.py:550
  254.2 5.2 assemble.3
  259.4 6.6 convolution_convert_fusion.4.gate_ref
  266.0 15.4 %intra.1.yin_ref = f32[512,1536]{1,0:T(8,128)} custom-call(bf16[512,1536]{1,0:T(8,128)(2,1)} %get-tuple-element.65.x_ref, bf16[512,128]{1,0:T(8,128)(2,1)} %get-tuple-element.195.b_ref, bf16[512,128]{1,0:T(8,128)(2,1)} %get-tuple-element.194.c_ref, f32[512,128]{1,0:T(8,128)} %get-tuple-element.67.dt_ref, f32[512,128]{1,0:T(8,128)} %get-tuple-element.68.cs_ref, ...), custom_call_target="tpu_custom_call" | custom-call | tf_op jit(solution)/shard_map/intra/pallas_call | solution.py:484
  281.4 7.1 %fusion.60.db_ref = f32[512,1536]{1,0:T(8,128)} fusion(bf16[512,1536]{1,0:T(8,128)(2,1)} %param.19, bf16[1536,1536]{1,0:T(8,128)(2,1)} %all-gather.5.cloned.1.call-done), kind=kOutput, calls=%fused_computation.142 | convolution fusion | flops 2415919104 | bytes 9437184 | tf_op jit(solution)/shard_map/dot_general | solution.py:22
  289.3 6.8 %stats.1 = (f32[512,1536]{1,0:T(8,128)}, f32[512,2]{1,0:T(8,128)}) custom-call(f32[512,1536]{1,0:T(8,128)} %intra.1.yin_ref, bf16[512,1536]{1,0:T(8,128)(2,1)} %get-tuple-element.65.x_ref, bf16[512,128]{1,0:T(8,128)(2,1)} %get-tuple-element.194.c_ref, f32[512,128]{1,0:T(8,128)} %get-tuple-element.68.cs_ref, bf16[16,2,8,1536]{3,2,1,0:T(8,128)(2,1)} %copy-done.3, ...), custom_call_target="tpu_custom_call" | custom-call | tf_op jit(solution)/shard_map/stats/pallas_call | solution.py:484
  296.1 2.4 all-gather
  299.3 8.4 %gate.1 = (bf16[512,1536]{1,0:T(8,128)(2,1)}, bf16[512,1536]{1,0:T(8,128)(2,1)}, bf16[512,1536]{1,0:T(8,128)(2,1)}, f32[2,1,1536]{2,1,0:T(1,128)}, bf16[16,2,8,1536]{3,2,1,0:T(8,128)(2,1)}) custom-call(f32[512,1536]{1,0:T(8,128)} %get-tuple-element.70.y_ref, bf16[512,128]{1,0:T(8,128)(2,1)} %get-tuple-element.194.c_ref, ...), custom_call_target="tpu_custom_call" | custom-call | tf_op jit(solution)/shard_map/gate/pallas_call | solution.py:484
  307.6 29.2 %all_to_all.35.refs_2_ = bf16[16,2,8,1536]{3,2,1,0:T(8,128)(2,1)} all-to-all(bf16[16,2,8,1536]{3,2,1,0:T(8,128)(2,1)} %get-tuple-element.75), channel_id=1, replica_groups=mesh['seq'=16,'head'=2] {'seq'}, dimensions={0} | all-to-all | bytes 1572864 | tf_op jit(solution)/shard_map/all_to_all | solution.py:550
  336.8 3.5 scan_back.1
  340.3 3.6 all-to-all-start.5
  344.2 23.3 %intra_back.1 = (f32[512,1536]{1,0:T(8,128)}, f32[512,128]{1,0:T(8,128)}, f32[512,128]{1,0:T(8,128)}, f32[512,128]{1,0:T(8,128)}, f32[512,128]{1,0:T(8,128)}, /*index=5*/f32[2,1,1536]{2,1,0:T(1,128)}) custom-call(bf16[512,1536]{1,0:T(8,128)(2,1)} %get-tuple-element.65.x_ref, bf16[512,1536]{1,0:T(8,128)(2,1)} %get-tuple-element.76.dy_ref, ...), custom_call_target="tpu_custom_call" | custom-call | tf_op jit(solution)/shard_map/intra_back/pallas_call | solution.py:484
  368.4 15.8 %state_back.1 = (bf16[528,1536]{1,0:T(8,128)(2,1)}, bf16[512,256]{1,0:T(8,128)(2,1)}, bf16[528,128]{1,0:T(8,128)(2,1)}, f32[2,4,1536]{2,1,0:T(4,128)}, f32[2,1,1...) custom-call(f32[2]{0:T(128)} %broadcast_subtract_fusion.keep_ref, ...), custom_call_target="tpu_custom_call" | custom-call | tf_op jit(solution)/shard_map/state_back/pallas_call | solution.py:484
  387.5 7.5 %reduce-scatter.10.cloned.1.call-done = bf16[128,512]{1,0:T(8,128)(2,1)} async-done(((bf16[256,512]{1,0:T(8,128)(2,1)}), bf16[128,512]{1,0:T(8,128)(2,1)}) %reduce-scatter.10.cloned.1.call-update) | async-done | bytes 131088
  396.7 2.7 bc_back.1
  401.3 5.8 fusion.61
  409.7 6.8 %all-to-all-start.6 = ((bf16[16,6,1536]{2,1,0:T(8,128)(2,1)}), bf16[16,6,1536]{2,1,0:T(8,128)(2,1)S(1)}, u32[]{:S(2)}, u32[]{:S(2)}) async-start(bf16[16,6,1536]{2,1,0:T(8,128)(2,1)} %broadcast_in_dim.84), calls=%async_computation.7 | async-start | bytes 786432 | tf_op jit(solution)/shard_map/all_to_all | solution.py:550
  421.0 8.6 %all-to-all-done.6 = bf16[16,6,1536]{2,1,0:T(8,128)(2,1)S(1)} async-done(((bf16[16,6,1536]{2,1,0:T(8,128)(2,1)}), bf16[16,6,1536]{2,1,0:T(8,128)(2,1)S(1)}, u32[]{:S(2)}, u32[]{:S(2)}) %all-to-all-start.6) | async-done | bytes 294944 | tf_op jit(solution)/shard_map/all_to_all | solution.py:550
  433.2 6.1 fusion.4
  441.0 5.7 convolution_convert_fusion
  446.7 5.4 take_apart.5
  452.1 2.6 copy.68
  457.3 4.4 convolution_convert_fusion.2
  461.7 5.3 take_apart.3
  467.0 2.5 copy.64
  473.2 6.1 convolution_convert_fusion.3
  479.3 4.6 collective-permute-done.46
  488.4 20.7 %collective-permute-done.32 = bf16[2,2,96,1536]{3,2,0,1:T(8,128)(2,1)} collective-permute-done((bf16[2,2,96,1536]{3,2,0,1:T(8,128)(2,1)}, bf16[2,2,96,1536]{3,2,0,1:T(8,128)(2,1)}, u32[]{:S(2)}, u32[]{:S(2)}) %collective-permute-start.32) | collective-permute-done | bytes 1179680 | tf_op jit(solution)/shard_map/ppermute | solution.py:544
  512.4 11.2 %collective-permute-done.47 = bf16[2,96,1536]{2,1,0:T(8,128)(2,1)S(1)} collective-permute-done((bf16[2,96,1536]{2,1,0:T(8,128)(2,1)S(1)}, bf16[2,96,1536]{2,1,0:T(8,128)(2,1)S(1)}, u32[]{:S(2)}, u32[]{:S(2)}) %collective-permute-start.47) | collective-permute-done | bytes 589856 | tf_op jit(solution)/shard_map/ppermute | solution.py:544
  527.0 2.7 collective-permute-start.50
  537.5 6.3 convolution_convert_fusion.1
  543.8 5.8 take_apart.4
  549.6 2.7 copy.66
  563.6 18.9 %collective-permute-done.39 = bf16[2,2,96,1792]{3,2,0,1:T(8,128)(2,1)} collective-permute-done((bf16[2,2,96,1792]{3,2,0,1:T(8,128)(2,1)}, bf16[2,2,96,1792]{3,2,0,1:T(8,128)(2,1)}, u32[]{:S(2)}, u32[]{:S(2)}) %collective-permute-start.39) | collective-permute-done | bytes 1376288 | tf_op jit(solution)/shard_map/ppermute | solution.py:544
  582.5 2.4 fusion.13
  585.1 8.2 %collective-permute-done.37 = bf16[2,2,96,1792]{3,2,0,1:T(8,128)(2,1)} collective-permute-done((bf16[2,2,96,1792]{3,2,0,1:T(8,128)(2,1)}, bf16[2,2,96,1792]{3,2,0,1:T(8,128)(2,1)}, u32[]{:S(2)}, u32[]{:S(2)}) %collective-permute-start.37) | collective-permute-done | bytes 1376288 | tf_op jit(solution)/shard_map/ppermute | solution.py:544
  595.5 8.9 %collective-permute-done.40 = bf16[2,96,1792]{2,1,0:T(8,128)(2,1)} collective-permute-done((bf16[2,96,1792]{2,1,0:T(8,128)(2,1)}, bf16[2,96,1792]{2,1,0:T(8,128)(2,1)}, u32[]{:S(2)}, u32[]{:S(2)}) %collective-permute-start.40) | collective-permute-done | bytes 688160 | tf_op jit(solution)/shard_map/ppermute | solution.py:544
  607.8 3.2 collective-permute-start.43
  620.3 2.4 collective-permute-done.43
  622.7 13.6 %collective-permute-done.42 = bf16[96,1792]{1,0:T(8,128)(2,1)S(1)} collective-permute-done((bf16[96,1792]{1,0:T(8,128)(2,1)}, bf16[96,1792]{1,0:T(8,128)(2,1)S(1)}, u32[]{:S(2)}, u32[]{:S(2)}) %collective-permute-start.42) | collective-permute-done | bytes 344096 | tf_op jit(solution)/shard_map/ppermute | solution.py:547
  641.5 4.0 collective-permute-done.53
  645.8 3.6 fusion.9
  (356 shorter events, 140.3 us)
Async XLA Ops:
  7.2 274.1 %all-gather.5.cloned.1.call-start = ((), (), s32[]{:S(2)}) async-start(), calls=%async_computation.10 | async-start | bytes 5013504 | tf_op jit(solution)/shard_map/all_gather | solution.py:597
  9.8 51.0 %collective-permute-start.7 = (bf16[96,1792]{1,0:T(8,128)(2,1)S(1)}, bf16[96,1792]{1,0:T(8,128)(2,1)}, u32[]{:S(2)}, u32[]{:S(2)}) collective-permute-start(bf16[96,1792]{1,0:T(8,128)(2,1)S(1)} %fusion.42.refs_0_), channel_id=1, source_target_pairs={{0,16},{2,18},{4,20},{6,22},{8,24},{10,26},{12,28},{14,30},{16,0},... | collective-permute-start | bytes 1032200 | tf_op jit(solution)/shard_map/ppermute | solution.py:547
  13.9 21.6 %collective-permute-start.11 = (bf16[96,1792]{1,0:T(8,128)(2,1)S(1)}, bf16[96,1792]{1,0:T(8,128)(2,1)S(1)}, u32[]{:S(2)}, u32[]{:S(2)}) collective-permute-start(bf16[96,1792]{1,0:T(8,128)(2,1)S(1)} %fusion.42.refs_0_), channel_id=1, source_target_pairs={{0,24},{2,26},{4,28},{6,30},{8,0},{10,2},{12,4},{14,6},{16,8},{18,... | collective-permute-start | bytes 1032200 | tf_op jit(solution)/shard_map/ppermute | solution.py:547
  15.2 48.0 %collective-permute-start.3 = (bf16[96,1792]{1,0:T(8,128)(2,1)S(1)}, bf16[96,1792]{1,0:T(8,128)(2,1)S(1)}, u32[]{:S(2)}, u32[]{:S(2)}) collective-permute-start(bf16[96,1792]{1,0:T(8,128)(2,1)S(1)} %fusion.42.refs_0_), channel_id=1, source_target_pairs={{0,8},{2,10},{4,12},{6,14},{8,16},{10,18},{12,20},{14,22},{16,24},... | collective-permute-start | bytes 1032200 | tf_op jit(solution)/shard_map/ppermute | solution.py:547
  15.9 47.8 %collective-permute-start.1 = (bf16[96,1792]{1,0:T(8,128)(2,1)S(1)}, bf16[96,1792]{1,0:T(8,128)(2,1)}, u32[]{:S(2)}, u32[]{:S(2)}) collective-permute-start(bf16[96,1792]{1,0:T(8,128)(2,1)S(1)} %fusion.42.refs_0_), channel_id=1, source_target_pairs={{0,4},{2,6},{4,0},{6,2},{8,12},{10,14},{12,8},{14,10},{16,20},{18,... | collective-permute-start | bytes 1032200 | tf_op jit(solution)/shard_map/ppermute | solution.py:544
  17.4 46.4 %collective-permute-start = (bf16[96,1792]{1,0:T(8,128)(2,1)S(1)}, bf16[96,1792]{1,0:T(8,128)(2,1)S(1)}, u32[]{:S(2)}, u32[]{:S(2)}) collective-permute-start(bf16[96,1792]{1,0:T(8,128)(2,1)S(1)} %fusion.42.refs_0_), channel_id=1, source_target_pairs={{0,2},{2,0},{4,6},{6,4},{8,10},{10,8},{12,14},{14,12},{16,18},{18,... | collective-permute-start | bytes 1032200 | tf_op jit(solution)/shard_map/ppermute | solution.py:544
  20.5 40.1 %all-to-all-start = ((bf16[16,6,1536]{2,1,0:T(8,128)(2,1)}), bf16[16,6,1536]{2,1,0:T(8,128)(2,1)S(1)}, u32[]{:S(2)}, u32[]{:S(2)}) async-start(bf16[16,6,1536]{2,1,0:T(8,128)(2,1)} %broadcast_in_dim.43), calls=%async_computation | async-start | bytes 786432 | tf_op jit(solution)/shard_map/all_to_all | solution.py:550
  35.5 49.8 %collective-permute-start.12 = (bf16[96,1792]{1,0:T(8,128)(2,1)S(1)}, bf16[96,1792]{1,0:T(8,128)(2,1)}, u32[]{:S(2)}, u32[]{:S(2)}) collective-permute-start(bf16[96,1792]{1,0:T(8,128)(2,1)S(1)} %collective-permute-done.11.refs_12_), channel_id=1, source_target_pairs={{0,2},{2,0},{4,6},{6,4},{8,10},{10,8},{12,14},{14,12},{16,18},{18,... | collective-permute-start | bytes 1032200 | tf_op jit(solution)/shard_map/ppermute | solution.py:544
  60.8 26.5 %collective-permute-start.13 = (bf16[96,1792]{1,0:T(8,128)(2,1)S(1)}, bf16[96,1792]{1,0:T(8,128)(2,1)S(1)}, u32[]{:S(2)}, u32[]{:S(2)}) collective-permute-start(bf16[96,1792]{1,0:T(8,128)(2,1)S(1)} %collective-permute-done.11.refs_12_), channel_id=1, source_target_pairs={{0,4},{2,6},{4,0},{6,2},{8,12},{10,14},{12,8},{14,10},{16,20},{18,... | collective-permute-start | bytes 1032200 | tf_op jit(solution)/shard_map/ppermute | solution.py:544
  63.2 22.8 %collective-permute-start.4 = (bf16[96,1792]{1,0:T(8,128)(2,1)S(1)}, bf16[96,1792]{1,0:T(8,128)(2,1)S(1)}, u32[]{:S(2)}, u32[]{:S(2)}) collective-permute-start(bf16[96,1792]{1,0:T(8,128)(2,1)S(1)} %collective-permute-done.3.refs_4_), channel_id=1, source_target_pairs={{0,2},{2,0},{4,6},{6,4},{8,10},{10,8},{12,14},{14,12},{16,18},{18,... | collective-permute-start | bytes 1032200 | tf_op jit(solution)/shard_map/ppermute | solution.py:544
  63.7 24.3 %collective-permute-start.5 = (bf16[96,1792]{1,0:T(8,128)(2,1)S(1)}, bf16[96,1792]{1,0:T(8,128)(2,1)S(1)}, u32[]{:S(2)}, u32[]{:S(2)}) collective-permute-start(bf16[96,1792]{1,0:T(8,128)(2,1)S(1)} %collective-permute-done.3.refs_4_), channel_id=1, source_target_pairs={{0,4},{2,6},{4,0},{6,2},{8,12},{10,14},{12,8},{14,10},{16,20},{18,... | collective-permute-start | bytes 1032200 | tf_op jit(solution)/shard_map/ppermute | solution.py:544
  63.8 20.1 %collective-permute-start.9 = (bf16[96,1792]{1,0:T(8,128)(2,1)}, bf16[96,1792]{1,0:T(8,128)(2,1)S(1)}, u32[]{:S(2)}, u32[]{:S(2)}) collective-permute-start(bf16[96,1792]{1,0:T(8,128)(2,1)} %collective-permute-done.7.refs_8_), channel_id=1, source_target_pairs={{0,4},{2,6},{4,0},{6,2},{8,12},{10,14},{12,8},{14,10},{16,20},{18,... | collective-permute-start | bytes 1032200 | tf_op jit(solution)/shard_map/ppermute | solution.py:544
  83.9 18.2 %collective-permute-start.8 = (bf16[96,1792]{1,0:T(8,128)(2,1)}, bf16[96,1792]{1,0:T(8,128)(2,1)S(1)}, u32[]{:S(2)}, u32[]{:S(2)}) collective-permute-start(bf16[96,1792]{1,0:T(8,128)(2,1)} %collective-permute-done.7.refs_8_), channel_id=1, source_target_pairs={{0,2},{2,0},{4,6},{6,4},{8,10},{10,8},{12,14},{14,12},{16,18},{18,... | collective-permute-start | bytes 1032200 | tf_op jit(solution)/shard_map/ppermute | solution.py:544
  85.3 31.6 %collective-permute-start.2 = (bf16[96,1792]{1,0:T(8,128)(2,1)}, bf16[96,1792]{1,0:T(8,128)(2,1)S(1)}, u32[]{:S(2)}, u32[]{:S(2)}) collective-permute-start(bf16[96,1792]{1,0:T(8,128)(2,1)} %collective-permute-done.1.refs_2_), channel_id=1, source_target_pairs={{0,2},{2,0},{4,6},{6,4},{8,10},{10,8},{12,14},{14,12},{16,18},{18,... | collective-permute-start | bytes 1032200 | tf_op jit(solution)/shard_map/ppermute | solution.py:544
  86.0 37.4 %collective-permute-start.10 = (bf16[96,1792]{1,0:T(8,128)(2,1)S(1)}, bf16[96,1792]{1,0:T(8,128)(2,1)S(1)}, u32[]{:S(2)}, u32[]{:S(2)}) collective-permute-start(bf16[96,1792]{1,0:T(8,128)(2,1)S(1)} %collective-permute-done.9.refs_10_), channel_id=1, source_target_pairs={{0,2},{2,0},{4,6},{6,4},{8,10},{10,8},{12,14},{14,12},{16,18},{18,... | collective-permute-start | bytes 1032200 | tf_op jit(solution)/shard_map/ppermute | solution.py:544
  87.3 36.0 %collective-permute-start.14 = (bf16[96,1792]{1,0:T(8,128)(2,1)}, bf16[96,1792]{1,0:T(8,128)(2,1)S(1)}, u32[]{:S(2)}, u32[]{:S(2)}) collective-permute-start(bf16[96,1792]{1,0:T(8,128)(2,1)} %collective-permute-done.12.refs_13_), channel_id=1, source_target_pairs={{0,4},{2,6},{4,0},{6,2},{8,12},{10,14},{12,8},{14,10},{16,20},{18,... | collective-permute-start | bytes 1032200 | tf_op jit(solution)/shard_map/ppermute | solution.py:544
  88.0 36.8 %collective-permute-start.6 = (bf16[96,1792]{1,0:T(8,128)(2,1)S(1)}, bf16[96,1792]{1,0:T(8,128)(2,1)}, u32[]{:S(2)}, u32[]{:S(2)}) collective-permute-start(bf16[96,1792]{1,0:T(8,128)(2,1)S(1)} %collective-permute-done.4.refs_5_), channel_id=1, source_target_pairs={{0,4},{2,6},{4,0},{6,2},{8,12},{10,14},{12,8},{14,10},{16,20},{18,... | collective-permute-start | bytes 1032200 | tf_op jit(solution)/shard_map/ppermute | solution.py:544
  139.8 27.7 %all-to-all-start.2 = ((f32[16,2,128]{2,1,0:T(2,128)}), f32[16,2,128]{2,1,0:T(2,128)S(1)}, u32[]{:S(2)}, u32[]{:S(2)}) async-start(f32[16,2,128]{2,1,0:T(2,128)} %broadcast_in_dim.81), calls=%async_computation.2 | async-start | bytes 32768 | tf_op jit(solution)/shard_map/all_to_all | solution.py:550
  167.5 70.9 %all-to-all-start.1 = ((bf16[16,2,8,1536]{3,2,1,0:T(8,128)(2,1)}), bf16[16,2,8,1536]{3,2,1,0:T(8,128)(2,1)S(1)}, u32[]{:S(2)}, u32[]{:S(2)}) async-start(bf16[16,2,8,1536]{3,2,1,0:T(8,128)(2,1)} %end_state.1), calls=%async_computation.1 | async-start | bytes 1572864 | tf_op jit(solution)/shard_map/all_to_all | solution.py:550
  174.4 24.4 %collective-permute-start.18 = (bf16[96,1536]{1,0:T(8,128)(2,1)S(1)}, bf16[96,1536]{1,0:T(8,128)(2,1)S(1)}, u32[]{:S(2)}, u32[]{:S(2)}) collective-permute-start(bf16[96,1536]{1,0:T(8,128)(2,1)S(1)} %copy-done.39), channel_id=1, source_target_pairs={{0,8},{2,10},{4,12},{6,14},{8,16},{10,18},{12,20},{14,22},{16,24},... | collective-permute-start | bytes 884744 | tf_op jit(solution)/shard_map/ppermute | solution.py:547
  176.4 38.3 %collective-permute-start.22 = (bf16[96,1536]{1,0:T(8,128)(2,1)S(1)}, bf16[96,1536]{1,0:T(8,128)(2,1)S(1)}, u32[]{:S(2)}, u32[]{:S(2)}) collective-permute-start(bf16[96,1536]{1,0:T(8,128)(2,1)S(1)} %copy-done.39), channel_id=1, source_target_pairs={{0,16},{2,18},{4,20},{6,22},{8,24},{10,26},{12,28},{14,30},{16,0},... | collective-permute-start | bytes 884744 | tf_op jit(solution)/shard_map/ppermute | solution.py:547
  178.8 37.4 %collective-permute-start.26 = (bf16[96,1536]{1,0:T(8,128)(2,1)S(1)}, bf16[96,1536]{1,0:T(8,128)(2,1)S(1)}, u32[]{:S(2)}, u32[]{:S(2)}) collective-permute-start(bf16[96,1536]{1,0:T(8,128)(2,1)S(1)} %copy-done.39), channel_id=1, source_target_pairs={{0,24},{2,26},{4,28},{6,30},{8,0},{10,2},{12,4},{14,6},{16,8},{18,... | collective-permute-start | bytes 884744 | tf_op jit(solution)/shard_map/ppermute | solution.py:547
  180.2 37.5 %collective-permute-start.16 = (bf16[96,1536]{1,0:T(8,128)(2,1)S(1)}, bf16[96,1536]{1,0:T(8,128)(2,1)}, u32[]{:S(2)}, u32[]{:S(2)}) collective-permute-start(bf16[96,1536]{1,0:T(8,128)(2,1)S(1)} %copy-done.39), channel_id=1, source_target_pairs={{0,4},{2,6},{4,0},{6,2},{8,12},{10,14},{12,8},{14,10},{16,20},{18,... | collective-permute-start | bytes 884744 | tf_op jit(solution)/shard_map/ppermute | solution.py:544
  181.7 36.6 %collective-permute-start.15 = (bf16[96,1536]{1,0:T(8,128)(2,1)S(1)}, bf16[96,1536]{1,0:T(8,128)(2,1)S(1)}, u32[]{:S(2)}, u32[]{:S(2)}) collective-permute-start(bf16[96,1536]{1,0:T(8,128)(2,1)S(1)} %copy-done.39), channel_id=1, source_target_pairs={{0,2},{2,0},{4,6},{6,4},{8,10},{10,8},{12,14},{14,12},{16,18},{18,... | collective-permute-start | bytes 884744 | tf_op jit(solution)/shard_map/ppermute | solution.py:544
  198.9 20.0 %collective-permute-start.19 = (bf16[96,1536]{1,0:T(8,128)(2,1)S(1)}, bf16[96,1536]{1,0:T(8,128)(2,1)}, u32[]{:S(2)}, u32[]{:S(2)}) collective-permute-start(bf16[96,1536]{1,0:T(8,128)(2,1)S(1)} %collective-permute-done.18.refs_4_), channel_id=1, source_target_pairs={{0,2},{2,0},{4,6},{6,4},{8,10},{10,8},{12,14},{14,12},{16,18},{18,... | collective-permute-start | bytes 884744 | tf_op jit(solution)/shard_map/ppermute | solution.py:544
  214.8 10.0 %collective-permute-start.24 = (bf16[96,1536]{1,0:T(8,128)(2,1)S(1)}, bf16[96,1536]{1,0:T(8,128)(2,1)}, u32[]{:S(2)}, u32[]{:S(2)}) collective-permute-start(bf16[96,1536]{1,0:T(8,128)(2,1)S(1)} %collective-permute-done.22.refs_8_), channel_id=1, source_target_pairs={{0,4},{2,6},{4,0},{6,2},{8,12},{10,14},{12,8},{14,10},{16,20},{18,... | collective-permute-start | bytes 884744 | tf_op jit(solution)/shard_map/ppermute | solution.py:544
  216.2 10.1 %collective-permute-start.27 = (bf16[96,1536]{1,0:T(8,128)(2,1)S(1)}, bf16[96,1536]{1,0:T(8,128)(2,1)}, u32[]{:S(2)}, u32[]{:S(2)}) collective-permute-start(bf16[96,1536]{1,0:T(8,128)(2,1)S(1)} %collective-permute-done.26.refs_12_), channel_id=1, source_target_pairs={{0,2},{2,0},{4,6},{6,4},{8,10},{10,8},{12,14},{14,12},{16,18},{18,... | collective-permute-start | bytes 884744 | tf_op jit(solution)/shard_map/ppermute | solution.py:544
  217.7 13.3 %collective-permute-start.20 = (bf16[96,1536]{1,0:T(8,128)(2,1)S(1)}, bf16[96,1536]{1,0:T(8,128)(2,1)S(1)}, u32[]{:S(2)}, u32[]{:S(2)}) collective-permute-start(bf16[96,1536]{1,0:T(8,128)(2,1)S(1)} %collective-permute-done.18.refs_4_), channel_id=1, source_target_pairs={{0,4},{2,6},{4,0},{6,2},{8,12},{10,14},{12,8},{14,10},{16,20},{18,... | collective-permute-start | bytes 884744 | tf_op jit(solution)/shard_map/ppermute | solution.py:544
  218.3 14.2 %collective-permute-start.23 = (bf16[96,1536]{1,0:T(8,128)(2,1)S(1)}, bf16[96,1536]{1,0:T(8,128)(2,1)S(1)}, u32[]{:S(2)}, u32[]{:S(2)}) collective-permute-start(bf16[96,1536]{1,0:T(8,128)(2,1)S(1)} %collective-permute-done.22.refs_8_), channel_id=1, source_target_pairs={{0,2},{2,0},{4,6},{6,4},{8,10},{10,8},{12,14},{14,12},{16,18},{18,... | collective-permute-start | bytes 884744 | tf_op jit(solution)/shard_map/ppermute | solution.py:544
  218.8 35.2 %collective-permute-start.28 = (bf16[96,1536]{1,0:T(8,128)(2,1)S(1)}, bf16[96,1536]{1,0:T(8,128)(2,1)}, u32[]{:S(2)}, u32[]{:S(2)}) collective-permute-start(bf16[96,1536]{1,0:T(8,128)(2,1)S(1)} %collective-permute-done.26.refs_12_), channel_id=1, source_target_pairs={{0,4},{2,6},{4,0},{6,2},{8,12},{10,14},{12,8},{14,10},{16,20},{18,... | collective-permute-start | bytes 884744 | tf_op jit(solution)/shard_map/ppermute | solution.py:544
  224.8 29.3 %collective-permute-start.17 = (bf16[96,1536]{1,0:T(8,128)(2,1)}, bf16[96,1536]{1,0:T(8,128)(2,1)}, u32[]{:S(2)}, u32[]{:S(2)}) collective-permute-start(bf16[96,1536]{1,0:T(8,128)(2,1)} %collective-permute-done.16.refs_2_), channel_id=1, source_target_pairs={{0,2},{2,0},{4,6},{6,4},{8,10},{10,8},{12,14},{14,12},{16,18},{18,... | collective-permute-start | bytes 884744 | tf_op jit(solution)/shard_map/ppermute | solution.py:544
  226.3 27.8 %collective-permute-start.21 = (bf16[96,1536]{1,0:T(8,128)(2,1)}, bf16[96,1536]{1,0:T(8,128)(2,1)}, u32[]{:S(2)}, u32[]{:S(2)}) collective-permute-start(bf16[96,1536]{1,0:T(8,128)(2,1)} %collective-permute-done.19.refs_5_), channel_id=1, source_target_pairs={{0,4},{2,6},{4,0},{6,2},{8,12},{10,14},{12,8},{14,10},{16,20},{18,... | collective-permute-start | bytes 884744 | tf_op jit(solution)/shard_map/ppermute | solution.py:544
  231.0 23.1 %collective-permute-start.25 = (bf16[96,1536]{1,0:T(8,128)(2,1)}, bf16[96,1536]{1,0:T(8,128)(2,1)}, u32[]{:S(2)}, u32[]{:S(2)}) collective-permute-start(bf16[96,1536]{1,0:T(8,128)(2,1)} %collective-permute-done.24.refs_10_), channel_id=1, source_target_pairs={{0,2},{2,0},{4,6},{6,4},{8,10},{10,8},{12,14},{14,12},{16,18},{18,... | collective-permute-start | bytes 884744 | tf_op jit(solution)/shard_map/ppermute | solution.py:544
  232.5 21.6 %collective-permute-start.29 = (bf16[96,1536]{1,0:T(8,128)(2,1)}, bf16[96,1536]{1,0:T(8,128)(2,1)}, u32[]{:S(2)}, u32[]{:S(2)}) collective-permute-start(bf16[96,1536]{1,0:T(8,128)(2,1)} %collective-permute-done.27.refs_13_), channel_id=1, source_target_pairs={{0,4},{2,6},{4,0},{6,2},{8,12},{10,14},{12,8},{14,10},{16,20},{18,... | collective-permute-start | bytes 884744 | tf_op jit(solution)/shard_map/ppermute | solution.py:544
  242.9 45.6 %all-to-all-start.3 = ((bf16[16,2,8,1536]{3,2,1,0:T(8,128)(2,1)}), bf16[16,2,8,1536]{3,2,1,0:T(8,128)(2,1)S(1)}, u32[]{:S(2)}, u32[]{:S(2)}) async-start(bf16[16,2,8,1536]{3,2,1,0:T(8,128)(2,1)} %scan.1), calls=%async_computation.3 | async-start | bytes 1572864 | tf_op jit(solution)/shard_map/all_to_all | solution.py:550
  340.3 27.2 %all-to-all-start.5 = ((bf16[16,2,8,1536]{3,2,1,0:T(8,128)(2,1)}), bf16[16,2,8,1536]{3,2,1,0:T(8,128)(2,1)S(1)}, u32[]{:S(2)}, u32[]{:S(2)}) async-start(bf16[16,2,8,1536]{3,2,1,0:T(8,128)(2,1)} %scan_back.1), calls=%async_computation.6 | async-start | bytes 1572864 | tf_op jit(solution)/shard_map/all_to_all | solution.py:550
  343.9 51.2 %reduce-scatter.10.cloned.1.call-start = ((), (), s32[]{:S(2)}) async-start(), calls=%async_computation.13 | async-start | bytes 393216
  409.7 19.9 %all-to-all-start.6 = ((bf16[16,6,1536]{2,1,0:T(8,128)(2,1)}), bf16[16,6,1536]{2,1,0:T(8,128)(2,1)S(1)}, u32[]{:S(2)}, u32[]{:S(2)}) async-start(bf16[16,6,1536]{2,1,0:T(8,128)(2,1)} %broadcast_in_dim.84), calls=%async_computation.7 | async-start | bytes 786432 | tf_op jit(solution)/shard_map/all_to_all | solution.py:550
  416.4 196.7 %reduce-scatter.8.cloned.1.call-start = ((), (), s32[]{:S(2)}) async-start(), calls=%async_computation.12 | async-start | bytes 2359296 | tf_op jit(solution)/shard_map/reduce_scatter | solution.py:777
  439.3 206.5 %reduce-scatter.6.cloned.1.call-start = ((), (), s32[]{:S(2)}) async-start(), calls=%async_computation.11 | async-start | bytes 2359296 | tf_op jit(solution)/shard_map/reduce_scatter | solution.py:719
  454.6 29.2 %collective-permute-start.46 = (bf16[2,2,96,1536]{3,2,0,1:T(8,128)(2,1)}, bf16[2,2,96,1536]{3,2,0,1:T(8,128)(2,1)}, u32[]{:S(2)}, u32[]{:S(2)}) collective-permute-start(bf16[2,2,96,1536]{3,2,0,1:T(8,128)(2,1)} %copy.68), channel_id=1, source_target_pairs={{0,4},{2,6},{4,0},{6,2},{8,12},{10,14},{12,8},{14,10},{16,20},{18,... | collective-permute-start | bytes 3538952 | tf_op jit(solution)/shard_map/ppermute | solution.py:544
  456.6 29.6 %collective-permute-start.44 = (bf16[2,2,96,1536]{3,2,0,1:T(8,128)(2,1)}, bf16[2,2,96,1536]{3,2,0,1:T(8,128)(2,1)}, u32[]{:S(2)}, u32[]{:S(2)}) collective-permute-start(bf16[2,2,96,1536]{3,2,0,1:T(8,128)(2,1)} %copy.67), channel_id=1, source_target_pairs={{0,2},{2,0},{4,6},{6,4},{8,10},{10,8},{12,14},{14,12},{16,18},{18,... | collective-permute-start | bytes 3538952 | tf_op jit(solution)/shard_map/ppermute | solution.py:544
  469.5 39.7 %collective-permute-start.32 = (bf16[2,2,96,1536]{3,2,0,1:T(8,128)(2,1)}, bf16[2,2,96,1536]{3,2,0,1:T(8,128)(2,1)}, u32[]{:S(2)}, u32[]{:S(2)}) collective-permute-start(bf16[2,2,96,1536]{3,2,0,1:T(8,128)(2,1)} %copy.64), channel_id=1, source_target_pairs={{0,4},{2,6},{4,0},{6,2},{8,12},{10,14},{12,8},{14,10},{16,20},{18,... | collective-permute-start | bytes 3538952 | tf_op jit(solution)/shard_map/ppermute | solution.py:544
  471.7 39.4 %collective-permute-start.30 = (bf16[2,2,96,1536]{3,2,0,1:T(8,128)(2,1)}, bf16[2,2,96,1536]{3,2,0,1:T(8,128)(2,1)S(1)}, u32[]{:S(2)}, u32[]{:S(2)}) collective-permute-start(bf16[2,2,96,1536]{3,2,0,1:T(8,128)(2,1)} %copy.63), channel_id=1, source_target_pairs={{0,2},{2,0},{4,6},{6,4},{8,10},{10,8},{12,14},{14,12},{16,18},{18,... | collective-permute-start | bytes 3538952 | tf_op jit(solution)/shard_map/ppermute | solution.py:544
  485.3 38.3 %collective-permute-start.47 = (bf16[2,96,1536]{2,1,0:T(8,128)(2,1)S(1)}, bf16[2,96,1536]{2,1,0:T(8,128)(2,1)S(1)}, u32[]{:S(2)}, u32[]{:S(2)}) collective-permute-start(bf16[2,96,1536]{2,1,0:T(8,128)(2,1)S(1)} %fusion.18), channel_id=1, source_target_pairs={{0,2},{2,0},{4,6},{6,4},{8,10},{10,8},{12,14},{14,12},{16,18},{18,... | collective-permute-start | bytes 1769480 | tf_op jit(solution)/shard_map/ppermute | solution.py:544
  487.6 42.1 %collective-permute-start.45 = (bf16[2,96,1536]{2,1,0:T(8,128)(2,1)S(1)}, bf16[2,96,1536]{2,1,0:T(8,128)(2,1)S(1)}, u32[]{:S(2)}, u32[]{:S(2)}) collective-permute-start(bf16[2,96,1536]{2,1,0:T(8,128)(2,1)S(1)} %fusion.21), channel_id=1, source_target_pairs={{0,4},{2,6},{4,0},{6,2},{8,12},{10,14},{12,8},{14,10},{16,20},{18,... | collective-permute-start | bytes 1769480 | tf_op jit(solution)/shard_map/ppermute | solution.py:544
  510.4 22.9 %collective-permute-start.33 = (bf16[2,96,1536]{2,1,0:T(8,128)(2,1)S(1)}, bf16[2,96,1536]{2,1,0:T(8,128)(2,1)S(1)}, u32[]{:S(2)}, u32[]{:S(2)}) collective-permute-start(bf16[2,96,1536]{2,1,0:T(8,128)(2,1)S(1)} %fusion.23), channel_id=1, source_target_pairs={{0,2},{2,0},{4,6},{6,4},{8,10},{10,8},{12,14},{14,12},{16,18},{18,... | collective-permute-start | bytes 1769480 | tf_op jit(solution)/shard_map/ppermute | solution.py:544
  511.2 41.0 %collective-permute-start.31 = (bf16[2,96,1536]{2,1,0:T(8,128)(2,1)S(1)}, bf16[2,96,1536]{2,1,0:T(8,128)(2,1)}, u32[]{:S(2)}, u32[]{:S(2)}) collective-permute-start(bf16[2,96,1536]{2,1,0:T(8,128)(2,1)S(1)} %fusion.26), channel_id=1, source_target_pairs={{0,4},{2,6},{4,0},{6,2},{8,12},{10,14},{12,8},{14,10},{16,20},{18,... | collective-permute-start | bytes 1769480 | tf_op jit(solution)/shard_map/ppermute | solution.py:544
  525.9 31.5 %collective-permute-start.48 = (bf16[96,1536]{1,0:T(8,128)(2,1)}, bf16[96,1536]{1,0:T(8,128)(2,1)}, u32[]{:S(2)}, u32[]{:S(2)}) collective-permute-start(bf16[96,1536]{1,0:T(8,128)(2,1)} %get-tuple-element.186), channel_id=1, source_target_pairs={{0,8},{2,10},{4,12},{6,14},{8,16},{10,18},{12,20},{14,22},{16,24},... | collective-permute-start | bytes 884744 | tf_op jit(solution)/shard_map/ppermute | solution.py:547
  527.0 32.4 %collective-permute-start.50 = (bf16[96,1536]{1,0:T(8,128)(2,1)}, bf16[96,1536]{1,0:T(8,128)(2,1)}, u32[]{:S(2)}, u32[]{:S(2)}) collective-permute-start(bf16[96,1536]{1,0:T(8,128)(2,1)} %get-tuple-element.187), channel_id=1, source_target_pairs={{0,24},{2,26},{4,28},{6,30},{8,0},{10,2},{12,4},{14,6},{16,8},{18,... | collective-permute-start | bytes 884744 | tf_op jit(solution)/shard_map/ppermute | solution.py:547
  531.8 28.1 %collective-permute-start.49 = (bf16[96,1536]{1,0:T(8,128)(2,1)}, bf16[96,1536]{1,0:T(8,128)(2,1)}, u32[]{:S(2)}, u32[]{:S(2)}) collective-permute-start(bf16[96,1536]{1,0:T(8,128)(2,1)} %fusion.45), channel_id=1, source_target_pairs={{0,16},{2,18},{4,20},{6,22},{8,24},{10,26},{12,28},{14,30},{16,0},... | collective-permute-start | bytes 884744 | tf_op jit(solution)/shard_map/ppermute | solution.py:547
  535.6 79.4 %collective-permute-start.34 = (bf16[96,1536]{1,0:T(8,128)(2,1)}, bf16[96,1536]{1,0:T(8,128)(2,1)}, u32[]{:S(2)}, u32[]{:S(2)}) collective-permute-start(bf16[96,1536]{1,0:T(8,128)(2,1)} %get-tuple-element.188), channel_id=1, source_target_pairs={{0,8},{2,10},{4,12},{6,14},{8,16},{10,18},{12,20},{14,22},{16,24},... | collective-permute-start | bytes 884744 | tf_op jit(solution)/shard_map/ppermute | solution.py:547
  552.3 30.2 %collective-permute-start.39 = (bf16[2,2,96,1792]{3,2,0,1:T(8,128)(2,1)}, bf16[2,2,96,1792]{3,2,0,1:T(8,128)(2,1)}, u32[]{:S(2)}, u32[]{:S(2)}) collective-permute-start(bf16[2,2,96,1792]{3,2,0,1:T(8,128)(2,1)} %copy.66), channel_id=1, source_target_pairs={{0,4},{2,6},{4,0},{6,2},{8,12},{10,14},{12,8},{14,10},{16,20},{18,... | collective-permute-start | bytes 4128776 | tf_op jit(solution)/shard_map/ppermute | solution.py:544
  557.4 57.7 %collective-permute-start.36 = (bf16[96,1536]{1,0:T(8,128)(2,1)}, bf16[96,1536]{1,0:T(8,128)(2,1)}, u32[]{:S(2)}, u32[]{:S(2)}) collective-permute-start(bf16[96,1536]{1,0:T(8,128)(2,1)} %get-tuple-element.189), channel_id=1, source_target_pairs={{0,24},{2,26},{4,28},{6,30},{8,0},{10,2},{12,4},{14,6},{16,8},{18,... | collective-permute-start | bytes 884744 | tf_op jit(solution)/shard_map/ppermute | solution.py:547
  559.4 57.2 %collective-permute-start.35 = (bf16[96,1536]{1,0:T(8,128)(2,1)}, bf16[96,1536]{1,0:T(8,128)(2,1)}, u32[]{:S(2)}, u32[]{:S(2)}) collective-permute-start(bf16[96,1536]{1,0:T(8,128)(2,1)} %fusion.44), channel_id=1, source_target_pairs={{0,16},{2,18},{4,20},{6,22},{8,24},{10,26},{12,28},{14,30},{16,0},... | collective-permute-start | bytes 884744 | tf_op jit(solution)/shard_map/ppermute | solution.py:547
  559.9 33.4 %collective-permute-start.37 = (bf16[2,2,96,1792]{3,2,0,1:T(8,128)(2,1)}, bf16[2,2,96,1792]{3,2,0,1:T(8,128)(2,1)}, u32[]{:S(2)}, u32[]{:S(2)}) collective-permute-start(bf16[2,2,96,1792]{3,2,0,1:T(8,128)(2,1)} %copy.65), channel_id=1, source_target_pairs={{0,2},{2,0},{4,6},{6,4},{8,10},{10,8},{12,14},{14,12},{16,18},{18,... | collective-permute-start | bytes 4128776 | tf_op jit(solution)/shard_map/ppermute | solution.py:544
  584.8 19.5 %collective-permute-start.40 = (bf16[2,96,1792]{2,1,0:T(8,128)(2,1)}, bf16[2,96,1792]{2,1,0:T(8,128)(2,1)}, u32[]{:S(2)}, u32[]{:S(2)}) collective-permute-start(bf16[2,96,1792]{2,1,0:T(8,128)(2,1)} %fusion.13), channel_id=1, source_target_pairs={{0,2},{2,0},{4,6},{6,4},{8,10},{10,8},{12,14},{14,12},{16,18},{18,... | collective-permute-start | bytes 2064392 | tf_op jit(solution)/shard_map/ppermute | solution.py:544
  594.6 13.2 %collective-permute-start.38 = (bf16[2,96,1792]{2,1,0:T(8,128)(2,1)S(1)}, bf16[2,96,1792]{2,1,0:T(8,128)(2,1)S(1)}, u32[]{:S(2)}, u32[]{:S(2)}) collective-permute-start(bf16[2,96,1792]{2,1,0:T(8,128)(2,1)S(1)} %fusion.16), channel_id=1, source_target_pairs={{0,4},{2,6},{4,0},{6,2},{8,12},{10,14},{12,8},{14,10},{16,20},{18,... | collective-permute-start | bytes 2064392 | tf_op jit(solution)/shard_map/ppermute | solution.py:544
  606.9 13.4 %collective-permute-start.41 = (bf16[96,1792]{1,0:T(8,128)(2,1)}, bf16[96,1792]{1,0:T(8,128)(2,1)S(1)}, u32[]{:S(2)}, u32[]{:S(2)}) collective-permute-start(bf16[96,1792]{1,0:T(8,128)(2,1)} %get-tuple-element.184), channel_id=1, source_target_pairs={{0,8},{2,10},{4,12},{6,14},{8,16},{10,18},{12,20},{14,22},{16,24},... | collective-permute-start | bytes 1032200 | tf_op jit(solution)/shard_map/ppermute | solution.py:547
  607.8 14.9 %collective-permute-start.43 = (bf16[96,1792]{1,0:T(8,128)(2,1)}, bf16[96,1792]{1,0:T(8,128)(2,1)}, u32[]{:S(2)}, u32[]{:S(2)}) collective-permute-start(bf16[96,1792]{1,0:T(8,128)(2,1)} %get-tuple-element.185), channel_id=1, source_target_pairs={{0,24},{2,26},{4,28},{6,30},{8,0},{10,2},{12,4},{14,6},{16,8},{18,... | collective-permute-start | bytes 1032200 | tf_op jit(solution)/shard_map/ppermute | solution.py:547
  615.0 21.3 %collective-permute-start.42 = (bf16[96,1792]{1,0:T(8,128)(2,1)}, bf16[96,1792]{1,0:T(8,128)(2,1)S(1)}, u32[]{:S(2)}, u32[]{:S(2)}) collective-permute-start(bf16[96,1792]{1,0:T(8,128)(2,1)} %fusion.43), channel_id=1, source_target_pairs={{0,16},{2,18},{4,20},{6,22},{8,24},{10,26},{12,28},{14,30},{16,0},... | collective-permute-start | bytes 1032200 | tf_op jit(solution)/shard_map/ppermute | solution.py:547
  615.1 4.1 collective-permute-start.51
  619.2 22.1 %collective-permute-start.52 = (f32[88,128]{1,0:T(8,128)S(1)}, f32[88,128]{1,0:T(8,128)S(1)}, u32[]{:S(2)}, u32[]{:S(2)}) collective-permute-start(f32[88,128]{1,0:T(8,128)S(1)} %fusion.54), channel_id=1, source_target_pairs={{0,4},{2,6},{4,0},{6,2},{8,12},{10,14},{12,8},{14,10},{16,20},{18,... | collective-permute-start | bytes 135176 | tf_op jit(solution)/shard_map/ppermute | solution.py:544
  645.5 5.0 collective-permute-start.54
  (71 other events, 845.9 us)
Sparse Core Ops, SparseCore 0:
  10.8 118.3 all-gather.4
  386.1 8.9 reduce-scatter.9
  439.4 7.0 reduce-scatter.7
  479.4 7.2 reduce-scatter.5
